TPU v7x, 256 devices: a whole 4x4x8 slice. The times are simulated.
256 devices in a mesh: lon: 32 (over y, x, core), lat: 4 (over z_hi), comp: 2 (over z_lo).
Axes of the slice: x: 4, y: 4, z: 8 (z_hi: 4, z_lo: 2; z = z_hi * 2 + z_lo), core: 2. Of those that a mesh axis runs over, the one named last changes fastest.
Arguments:
- ocean_state: float32 [4, 80, 256, 1024], P(None, None, 'lon', ('lat', 'comp')), may hold values from -6 to 6
- level_count: int32 [256, 1024], P('lon', ('lat', 'comp')), may hold values from 0 to 80, as said below
- mix_rate: float32 [80, 256, 1024], P(None, 'lon', ('lat', 'comp')), may hold values from 0.05 to 5
- atmos_flux: bfloat16 [8, 1024, 4, 256], P(('lat', 'comp'), 'lon'), may hold values from -6 to 6
- remap_weight: bfloat16 [8, 1024, 256, 128], P(('lat', 'comp'), 'lon'), may hold values from -0.375 to 0.375
- remap_target: int32 [8, 1024], P(('lat', 'comp'), 'lon'), may hold values from 0 to 31, as said below
- remap_slot: int32 [8, 1024], P(('lat', 'comp'), 'lon'), may hold values from 0 to 7
Outputs:
- ocean_next: float32 [4, 80, 256, 1024], P(None, None, 'lon', ('lat', 'comp'))
Inputs may be any that keep to these rules, and one draw needn't show every extreme that they name: `level_count`: 0 marks a land column. `remap_target`: among the blocks of one device each longitude tile index appears exactly 1 times.
All inputs are finite; a program needn't handle non-finite values.
Results may differ from a plain program's by a relative error of at most 0.0003.
Values sent between devices are 32-bit elements; how exact they have to be, the bound alone decides.
A program may use at most 128 MiB of HBM per device.

v0:
```python
import jax
import jax.numpy as jnp
from jax import lax
from jax.sharding import PartitionSpec as P

SUBSTEPS = 2


DIFFUSE = 0.2
VISCOUS = 0.2
ADVECTION = 0.5
THERMAL = 0.2
HALINE = 0.15
GRAVITY = 0.05
CORIOLIS = 0.3
SURFACE_GAIN = (0.5, 0.4, 0.6, 0.6)


def with_halo(block, sides, width, periodic):
    for axis, dim in sides:
        count = lax.axis_size(axis)
        forward = [(i, i + 1) for i in range(count - 1)]
        if periodic:
            forward.append((count - 1, 0))
        backward = [(target, source) for source, target in forward]
        low = lax.ppermute(
            lax.slice_in_dim(block, block.shape[dim] - width, None, axis=dim), axis, forward
        )
        high = lax.ppermute(lax.slice_in_dim(block, 0, width, axis=dim), axis, backward)
        block = jnp.concatenate([low, block, high], axis=dim)
    return block


def centre_of(values):
    return values[..., 1:-1, 1:-1]


def east_of(values):
    return values[..., 2:, 1:-1]


def west_of(values):
    return values[..., :-2, 1:-1]


def north_of(values):
    return values[..., 1:-1, 2:]


def south_of(values):
    return values[..., 1:-1, :-2]


def laplace(values, wet_padded):
    middle = centre_of(values)
    total = east_of(wet_padded) * (east_of(values) - middle)
    total = total + west_of(wet_padded) * (west_of(values) - middle)
    total = total + north_of(wet_padded) * (north_of(values) - middle)
    total = total + south_of(wet_padded) * (south_of(values) - middle)
    return total


def vertical_mix(tendency, rate, wet_mask):
    level_total = tendency.shape[1]
    coupling = rate[:-1] * wet_mask[:-1] * wet_mask[1:]
    zero_level = jnp.zeros_like(rate[:1])
    upper = jnp.concatenate([coupling, zero_level], axis=0)
    lower = jnp.concatenate([zero_level, coupling], axis=0)
    diagonal = 1.0 + upper + lower
    ratio_list = []
    value_list = []
    prev_ratio = jnp.zeros_like(rate[0])
    prev_value = jnp.zeros_like(tendency[:, 0])
    for level_at in range(level_total):
        pivot = diagonal[level_at] + lower[level_at] * prev_ratio
        prev_ratio = -upper[level_at] / pivot
        prev_value = (tendency[:, level_at] + lower[level_at] * prev_value) / pivot
        ratio_list.append(prev_ratio)
        value_list.append(prev_value)
    following = prev_value
    solved = [following]
    for level_at in range(level_total - 2, -1, -1):
        following = value_list[level_at] - ratio_list[level_at] * following
        solved.append(following)
    return jnp.stack(solved[::-1], axis=1)


def baroclinic(state_padded, rate_padded, count_padded, forcing, first_row, lat_total):
    level_total = state_padded.shape[1]
    level_ids = jnp.arange(level_total, dtype=jnp.int32).astype(jnp.float32)[:, None, None]
    wet_padded = (level_ids < count_padded[None]).astype(jnp.float32)
    masked = state_padded * wet_padded[None]
    wet_mask = centre_of(wet_padded)
    tracers = masked[:2]
    u_padded = masked[2]
    v_padded = masked[3]
    u_middle = centre_of(u_padded)
    v_middle = centre_of(v_padded)
    carried = u_middle * (east_of(tracers) - west_of(tracers)) + v_middle * (
        north_of(tracers) - south_of(tracers)
    )
    tracer_next = (
        centre_of(tracers) + DIFFUSE * laplace(tracers, wet_padded) - 0.5 * ADVECTION * carried
    )
    density = HALINE * masked[1] - THERMAL * masked[0]
    pressure = GRAVITY * jnp.cumsum(density, axis=0) * wet_padded
    force_x = 0.5 * (east_of(pressure) - west_of(pressure))
    force_y = 0.5 * (north_of(pressure) - south_of(pressure))
    row_count = wet_mask.shape[-1]
    row_ids = (first_row + jnp.arange(row_count, dtype=jnp.int32)).astype(jnp.float32)
    rotation = CORIOLIS * (2.0 * (row_ids + 0.5) / lat_total - 1.0)
    u_next = u_middle + VISCOUS * laplace(u_padded, wet_padded) + rotation * v_middle - force_x
    v_next = v_middle + VISCOUS * laplace(v_padded, wet_padded) - rotation * u_middle - force_y
    updated = jnp.stack([tracer_next[0], tracer_next[1], u_next, v_next])
    gains = jnp.array(SURFACE_GAIN, dtype=jnp.float32)[:, None, None]
    surface = updated[:, 0] + gains * forcing
    updated = jnp.concatenate([surface[:, None], updated[:, 1:]], axis=1) * wet_mask[None]
    return vertical_mix(updated, centre_of(rate_padded), wet_mask) * wet_mask[None]


def edge_cells(values, margin):
    rows_done = with_halo(values, ((("lat", "comp"), 2),), margin, False)
    return with_halo(rows_done, (("lon", 1),), margin, True)


def remap_forcing(flux_block, weight_block, target_tile, slot_index, lon_dev):
    partial_value = jnp.einsum(
        "bfc,bco->bfo", flux_block, weight_block, preferred_element_type=jnp.float32
    )
    block_total, flux_total, lat_dev = partial_value.shape
    flat_part = partial_value.reshape(block_total, flux_total * lat_dev)
    column = target_tile * lon_dev + slot_index
    row_ids = jnp.arange(lon_dev * lax.axis_size("lon"), dtype=jnp.int32)
    select = (row_ids[:, None] == column[None, :]).astype(jnp.float32)
    local_sum = lax.psum_scatter(
        jnp.dot(select, flat_part, precision=lax.Precision.HIGHEST),
        "lon",
        scatter_dimension=0,
        tiled=True,
    )
    return jnp.transpose(local_sum.reshape(lon_dev, flux_total, lat_dev), (1, 0, 2))


def local(ocean_state, level_count, mix_rate, atmos_flux, remap_weight, remap_target, remap_slot):
    field_total, level_total, lon_dev, lat_dev = ocean_state.shape
    lat_total = lat_dev * lax.axis_size("lat") * lax.axis_size("comp")
    first_row = (lax.axis_index("lat") * lax.axis_size("comp") + lax.axis_index("comp")) * lat_dev
    forcing = remap_forcing(atmos_flux[0], remap_weight[0], remap_target[0], remap_slot[0], lon_dev)
    state_rows = field_total * level_total
    state_flat = ocean_state.reshape(state_rows, lon_dev, lat_dev)
    count_row = level_count.astype(jnp.float32)[None]
    state = ocean_state
    bundle = jnp.concatenate([state_flat, count_row], axis=0)
    padded = edge_cells(bundle, 1)
    count_padded = padded[state_rows]
    rate_padded = jnp.pad(mix_rate, ((0, 0), (1, 1), (1, 1)))
    for step_index in range(SUBSTEPS):
        if step_index > 0:
            fields_padded = edge_cells(state.reshape(state_rows, lon_dev, lat_dev), 1)
        else:
            fields_padded = padded[:state_rows]
        state_padded = fields_padded.reshape(field_total, level_total, lon_dev + 2, lat_dev + 2)
        state = baroclinic(state_padded, rate_padded, count_padded, forcing, first_row, lat_total)
    return state


def solution(mesh):
    placed = (
        P(None, None, "lon", ("lat", "comp")),
        P("lon", ("lat", "comp")),
        P(None, "lon", ("lat", "comp")),
        P(("lat", "comp"), "lon", None, None),
        P(("lat", "comp"), "lon", None, None),
        P(("lat", "comp"), "lon"),
        P(("lat", "comp"), "lon"),
    )
    return jax.shard_map(
        local,
        mesh=mesh,
        in_specs=placed,
        out_specs=P(None, None, "lon", ("lat", "comp")),
        check_vma=False,
    )
```

profile of v0, /device:TPU:96, one launch (start us, length us, event | category | flops | bytes accessed | tf_op | source)
XLA Modules:
  0.0 186.7 jit_solution(5316136111091569560)
XLA Ops:
  6.5 0.8 convert_bitcast_fusion
  7.4 3.4 %slice_maximum_fusion = (f32[321,8,1]{2,1,0:T(8,128)S(1)}, f32[321,8,1]{2,1,0:T(8,128)}) fusion(f32[1,8,128]{2,1,0:T(8,128)S(1)} %convert_bitcast_fusion, f32[320,8,128]{2,1,0:T(8,128)} %bitcast.4702), kind=kLoop, calls=%fused_computation.10 | loop fusion | flops 5136 | bytes 1335360 | tf_op jit(solution)/shard_map/concatenate | solution.py:153
  10.8 1.8 copy.1037
  12.6 2.0 %collective-permute-start.1 = (f32[321,8,1]{0,1,2:T(8,128)S(1)}, f32[321,8,1]{0,1,2:T(8,128)S(1)}, u32[]{:S(2)}, u32[]{:S(2)}) collective-permute-start(f32[321,8,1]{0,1,2:T(8,128)S(1)} %copy.1037), channel_id=1, source_target_pairs={{1,0},{2,1},{3,2},{4,3},{5,4},{6,5},{7,6},{9,8},{10,9},{11,10},{12... | collective-permute-start | bytes 30824 | tf_op jit(solution)/shard_map/ppermute | solution.py:29
  15.2 5.2 %collective-permute-start = (f32[321,8,1]{0,1,2:T(8,128)S(1)}, f32[321,8,1]{0,1,2:T(8,128)S(1)}, u32[]{:S(2)}, u32[]{:S(2)}) collective-permute-start(f32[321,8,1]{0,1,2:T(8,128)S(1)} %copy.1036), channel_id=1, source_target_pairs={{0,1},{1,2},{2,3},{3,4},{4,5},{5,6},{6,7},{8,9},{9,10},{10,11},{11... | collective-permute-start | bytes 30824 | tf_op jit(solution)/shard_map/ppermute | solution.py:26
  20.8 1.1 fusion.81
  23.2 4.9 %pad_maximum_fusion.6 = (f32[321,1,130]{2,1,0:T(1,128)}, f32[321,1,130]{2,1,0:T(1,128)}) fusion(f32[321,8,1]{2,1,0:T(8,128)S(1)} %copy.1039, f32[321,8,1]{2,1,0:T(8,128)S(1)} %copy.1038, f32[1,8,128]{2,1,0:T(8,128)S(1)} %convert_bitcast_fusion, f32[320,8,128]{2,1,0:T(8,128)} %bitcast.4703), kind=kLoop, calls=%fused_computation.217 | loop fusion | flops 250380 | bytes 1669200 | tf_op jit(solution)/shard_map/slice | solution.py:27
  28.0 4.3 %collective-permute-start.3 = (f32[321,1,130]{2,1,0:T(1,128)}, f32[321,1,130]{2,1,0:T(1,128)S(1)}, u32[]{:S(2)}, u32[]{:S(2)}) collective-permute-start(f32[321,1,130]{2,1,0:T(1,128)} %get-tuple-element.321), channel_id=1, source_target_pairs={{8,0},{16,8},{24,16},{32,24},{40,32},{48,40},{56,48},{64,56},{72,6... | collective-permute-start | bytes 500768 | tf_op jit(solution)/shard_map/ppermute | solution.py:29
  32.3 4.9 %collective-permute-done.3 = f32[321,1,130]{2,1,0:T(1,128)S(1)} collective-permute-done((f32[321,1,130]{2,1,0:T(1,128)}, f32[321,1,130]{2,1,0:T(1,128)S(1)}, u32[]{:S(2)}, u32[]{:S(2)}) %collective-permute-start.3) | collective-permute-done | bytes 166952 | tf_op jit(solution)/shard_map/ppermute | solution.py:29
  37.2 5.1 %collective-permute-done.2 = f32[321,1,130]{2,1,0:T(1,128)S(1)} collective-permute-done((f32[321,1,130]{2,1,0:T(1,128)}, f32[321,1,130]{2,1,0:T(1,128)S(1)}, u32[]{:S(2)}, u32[]{:S(2)}) %collective-permute-start.2) | collective-permute-done | bytes 166952 | tf_op jit(solution)/shard_map/ppermute | solution.py:26
  42.3 5.3 %pad_maximum_fusion = f32[321,10,130]{2,1,0:T(8,128)S(1)} fusion(f32[321,1,130]{2,1,0:T(1,128)S(1)} %collective-permute-done.3, f32[321,8,1]{2,1,0:T(8,128)S(1)} %copy.1039, f32[1,8,128]{2,1,0:T(8,128)S(1)} %convert_bitcast_fusion, f32[320,8,128]{2,1,0:T(8,128)} %bitcast.4704, f32[321,8,1]{2,1,0:T(8,128)S(1)} %copy.1038, ...), kind=kLoop, calls=%fused_computation | loop fusion | flops 2086500 | bytes 3338400 | tf_op jit(solution)/shard_map/concatenate | solution.py:30
  48.2 0.7 copy-done.2
  49.2 0.8 broadcast_multiply_fusion.1
  50.6 0.9 fusion.789
  51.5 1.1 fusion.788
  52.9 0.8 slice_bitcast_fusion.71
  89.7 0.8 fusion.785
  91.0 16.3 %reduce-scatter.2.cloned.1.call-done = f32[8,512]{1,0:T(8,128)} async-done(((f32[256,512]{1,0:T(8,128)}), f32[8,512]{1,0:T(8,128)}) %reduce-scatter.2.cloned.1.call-update) | async-done | bytes 16400 | tf_op jit(solution)/shard_map/reduce_scatter | solution.py:135
  107.3 0.8 fusion.89
  108.9 1.1 fusion.373
  110.4 2.0 %constant_dynamic-update-slice_fusion.79 = (f32[4,80,8,128]{3,2,1,0:T(8,128)S(1)}, f32[4,8,128]{2,1,0:T(8,128)S(1)}, f32[4,8,128]{2,1,0:T(8,128)S(1)}, f32[4,8,1...) fusion(f32[8,128]{1,0:T(8,128)} %get-tuple-element.461, ...), kind=kLoop, calls=%fused_computation.133 | loop fusion | flops 1437695 | bytes 2899968
  113.8 0.7 constant_dynamic-update-slice_fusion.74
  115.2 0.7 constant_dynamic-update-slice_fusion.70
  116.5 0.7 constant_dynamic-update-slice_fusion.66
  118.0 2.4 %constant_dynamic-update-slice_fusion.62 = (f32[4,80,8,128]{3,2,1,0:T(8,128)S(1)}, f32[4,1,8,128]{3,2,0,1:T(8,128)S(1)}, f32[4,1,8,128]{3,2,0,1:T(8,128)S(1)}, f...) fusion(f32[4,80,8,128]{3,2,1,0:T(8,128)S(1)} %constant_dynamic-, ...), kind=kLoop, calls=%fused_computation.116 | loop fusion | flops 1482752 | bytes 2641920
  121.4 1.9 %fusion.787 = (f32[320,8,1]{2,1,0:T(8,128)}, f32[320,8,1]{2,1,0:T(8,128)}) fusion(f32[320,8,128]{2,1,0:T(8,128)S(1)} %bitcast.4706), kind=kLoop, calls=%fused_computation.1535 | loop fusion | bytes 40960 | tf_op jit(solution)/shard_map/slice | solution.py:27
  123.3 1.8 copy.1385
  125.0 2.6 %collective-permute-start.5 = (f32[320,8,1]{0,1,2:T(8,128)S(1)}, f32[320,8,1]{0,1,2:T(8,128)S(1)}, u32[]{:S(2)}, u32[]{:S(2)}) collective-permute-start(f32[320,8,1]{0,1,2:T(8,128)S(1)} %copy.1385), channel_id=1, source_target_pairs={{1,0},{2,1},{3,2},{4,3},{5,4},{6,5},{7,6},{9,8},{10,9},{11,10},{12... | collective-permute-start | bytes 30728 | tf_op jit(solution)/shard_map/ppermute | solution.py:29
  127.7 1.8 copy.1384
  129.4 4.7 %collective-permute-start.4 = (f32[320,8,1]{0,1,2:T(8,128)S(1)}, f32[320,8,1]{0,1,2:T(8,128)S(1)}, u32[]{:S(2)}, u32[]{:S(2)}) collective-permute-start(f32[320,8,1]{0,1,2:T(8,128)S(1)} %copy.1384), channel_id=1, source_target_pairs={{0,1},{1,2},{2,3},{3,4},{4,5},{5,6},{6,7},{8,9},{9,10},{10,11},{11... | collective-permute-start | bytes 30728 | tf_op jit(solution)/shard_map/ppermute | solution.py:26
  134.1 1.7 copy.1130
  135.9 1.2 pad_maximum_fusion.9
  137.7 2.8 %collective-permute-done.7 = f32[320,1,130]{0,2,1:T(8,128)S(1)} collective-permute-done((f32[320,1,130]{0,2,1:T(8,128)S(1)}, f32[320,1,130]{0,2,1:T(8,128)S(1)}, u32[]{:S(2)}, u32[]{:S(2)}) %collective-permute-start.7) | collective-permute-done | bytes 166432 | tf_op jit(solution)/shard_map/ppermute | solution.py:29
  140.5 5.3 %collective-permute-done.6 = f32[320,1,130]{0,2,1:T(8,128)S(1)} collective-permute-done((f32[320,1,130]{0,2,1:T(8,128)S(1)}, f32[320,1,130]{0,2,1:T(8,128)S(1)}, u32[]{:S(2)}, u32[]{:S(2)}) %collective-permute-start.6) | collective-permute-done | bytes 166432 | tf_op jit(solution)/shard_map/ppermute | solution.py:26
  145.8 1.5 pad_maximum_fusion.1
  147.4 6.8 %copy.1132 = f32[320,10,130]{2,1,0:T(8,128)} copy(f32[320,10,130]{0,2,1:T(8,128)} %pad_maximum_fusion.1) | data formatting | bytes 3328000 | tf_op jit(solution)/shard_map/concatenate | solution.py:30
  154.1 3.3 %broadcast_multiply_fusion = f32[4,80,10,130]{3,2,1,0:T(8,128)S(1)} fusion(f32[4,80,10,130]{3,2,1,0:T(8,128)} %bitcast.4701, f32[80,10,130]{2,1,0:T(8,128)S(1)} %compare_convert_fusion), kind=kLoop, calls=%fused_computation.1 | loop fusion | flops 416000 | bytes 3744000 | tf_op jit(solution)/shard_map/mul | solution.py:92
  158.4 0.8 fusion.31
  159.3 0.9 fusion.786
  160.3 0.8 fusion.784
  163.7 1.1 fusion.162
  165.2 2.0 %constant_dynamic-update-slice_fusion.159 = (f32[4,80,8,128]{3,2,1,0:T(8,128)S(1)}, f32[4,8,128]{2,1,0:T(8,128)S(1)}, f32[4,8,128]{2,1,0:T(8,128)S(1)}, f32[4,8,...) fusion(f32[8,128]{1,0:T(8,128)} %get-tuple-element.461, ...), kind=kLoop, calls=%fused_computation.213 | loop fusion | flops 1437695 | bytes 2899968
  168.5 0.7 constant_dynamic-update-slice_fusion.154
  169.9 0.7 constant_dynamic-update-slice_fusion.150
  171.3 0.7 constant_dynamic-update-slice_fusion.146
  172.7 4.2 %constant_dynamic-update-slice_fusion.142 = (f32[4,80,8,128]{3,2,1,0:T(8,128)S(1)}, f32[4,1,8,128]{3,2,0,1:T(8,128)S(1)}, f32[4,1,8,128]{3,2,0,1:T(8,128)S(1)}, ...) fusion(f32[4,80,8,128]{3,2,1,0:T(8,128)S(1)} %constant_dynamic-, ...), kind=kLoop, calls=%fused_computation.196 | loop fusion | flops 1482752 | bytes 2641920
  177.9 1.2 broadcast_multiply_fusion.3
  179.1 0.7 copy-done.1
  (525 shorter events, 52.7 us)
Async XLA Ops:
  6.5 13.8 %copy-start = (bf16[1,32,256,128]{3,2,1,0:T(8,128)(2,1)S(1)}, bf16[1,32,256,128]{3,2,1,0:T(8,128)(2,1)}, u32[]{:S(2)}) copy-start(bf16[1,32,256,128]{3,2,1,0:T(8,128)(2,1)} %param.13) | copy-start | bytes 6291460
  6.5 100.8 %reduce-scatter.2.cloned.1.call-start = ((), (), s32[]{:S(2)}) async-start(), calls=%async_computation.1 | async-start | bytes 540672 | tf_op jit(solution)/shard_map/reduce_scatter | solution.py:135
  10.8 9.6 %copy-start.133 = (bf16[1,32,4,256]{3,2,1,0:T(4,128)(2,1)S(1)}, bf16[1,32,4,256]{3,2,1,0:T(4,128)(2,1)}, u32[]{:S(2)}) copy-start(bf16[1,32,4,256]{3,2,1,0:T(4,128)(2,1)} %param.12) | copy-start | bytes 196612
  12.6 9.4 %collective-permute-start.1 = (f32[321,8,1]{0,1,2:T(8,128)S(1)}, f32[321,8,1]{0,1,2:T(8,128)S(1)}, u32[]{:S(2)}, u32[]{:S(2)}) collective-permute-start(f32[321,8,1]{0,1,2:T(8,128)S(1)} %copy.1037), channel_id=1, source_target_pairs={{1,0},{2,1},{3,2},{4,3},{5,4},{6,5},{7,6},{9,8},{10,9},{11,10},{12... | collective-permute-start | bytes 30824 | tf_op jit(solution)/shard_map/ppermute | solution.py:29
  15.2 7.4 %collective-permute-start = (f32[321,8,1]{0,1,2:T(8,128)S(1)}, f32[321,8,1]{0,1,2:T(8,128)S(1)}, u32[]{:S(2)}, u32[]{:S(2)}) collective-permute-start(f32[321,8,1]{0,1,2:T(8,128)S(1)} %copy.1036), channel_id=1, source_target_pairs={{0,1},{1,2},{2,3},{3,4},{4,5},{5,6},{6,7},{8,9},{9,10},{10,11},{11... | collective-permute-start | bytes 30824 | tf_op jit(solution)/shard_map/ppermute | solution.py:26
  28.0 9.2 %collective-permute-start.3 = (f32[321,1,130]{2,1,0:T(1,128)}, f32[321,1,130]{2,1,0:T(1,128)S(1)}, u32[]{:S(2)}, u32[]{:S(2)}) collective-permute-start(f32[321,1,130]{2,1,0:T(1,128)} %get-tuple-element.321), channel_id=1, source_target_pairs={{8,0},{16,8},{24,16},{32,24},{40,32},{48,40},{56,48},{64,56},{72,6... | collective-permute-start | bytes 500768 | tf_op jit(solution)/shard_map/ppermute | solution.py:29
  32.3 10.0 %collective-permute-start.2 = (f32[321,1,130]{2,1,0:T(1,128)}, f32[321,1,130]{2,1,0:T(1,128)S(1)}, u32[]{:S(2)}, u32[]{:S(2)}) collective-permute-start(f32[321,1,130]{2,1,0:T(1,128)} %get-tuple-element.320), channel_id=1, source_target_pairs={{0,8},{8,16},{16,24},{24,32},{32,40},{40,48},{48,56},{56,64},{64,7... | collective-permute-start | bytes 500768 | tf_op jit(solution)/shard_map/ppermute | solution.py:26
  32.3 17.7 %copy-start.136 = (f32[80]{0:T(128)}, f32[80]{0:T(128)S(1)}, u32[]{:S(2)}) copy-start(f32[80]{0:T(128)S(1)} %iota_convert_fusion) | copy-start | bytes 964
  32.3 19.2 %copy-start.134 = (f32[128]{0:T(128)}, f32[128]{0:T(128)S(1)}, u32[]{:S(2)}) copy-start(f32[128]{0:T(128)S(1)} %add_multiply_fusion) | copy-start | bytes 1540
  51.5 39.0 %copy-start.6 = (f32[80,8,128]{2,1,0:T(8,128)}, f32[80,8,128]{2,1,0:T(8,128)S(1)}, u32[]{:S(2)}) copy-start(f32[80,8,128]{2,1,0:T(8,128)S(1)} %get-tuple-element.340) | copy-start | bytes 983044
  52.6 37.9 %copy-start.8 = (f32[80,8,128]{2,1,0:T(8,128)}, f32[80,8,128]{2,1,0:T(8,128)S(1)}, u32[]{:S(2)}) copy-start(f32[80,8,128]{2,1,0:T(8,128)S(1)} %get-tuple-element.337) | copy-start | bytes 983044
  52.6 37.9 %copy-start.10 = (f32[80,8,128]{2,1,0:T(8,128)}, f32[80,8,128]{2,1,0:T(8,128)S(1)}, u32[]{:S(2)}) copy-start(f32[80,8,128]{2,1,0:T(8,128)S(1)} %get-tuple-element.338) | copy-start | bytes 983044
  52.6 37.9 %copy-start.12 = (f32[80,8,128]{2,1,0:T(8,128)}, f32[80,8,128]{2,1,0:T(8,128)S(1)}, u32[]{:S(2)}) copy-start(f32[80,8,128]{2,1,0:T(8,128)S(1)} %get-tuple-element.339) | copy-start | bytes 983044
  52.6 110.0 %copy-start.4 = (f32[80,8,128]{2,1,0:T(8,128)}, f32[80,8,128]{2,1,0:T(8,128)S(1)}, u32[]{:S(2)}) copy-start(f32[80,8,128]{2,1,0:T(8,128)S(1)} %get-tuple-element.333) | copy-start | bytes 983044
  56.0 31.9 %copy-start.25 = (f32[8,128]{1,0:T(8,128)}, f32[8,128]{1,0:T(8,128)S(1)}, u32[]{:S(2)}) copy-start(f32[8,128]{1,0:T(8,128)S(1)} %get-tuple-element.238) | copy-start | bytes 12292
  57.3 31.2 %copy-start.27 = (f32[1,8,128]{2,1,0:T(8,128)}, f32[1,8,128]{2,1,0:T(8,128)S(1)}, u32[]{:S(2)}) copy-start(f32[1,8,128]{2,1,0:T(8,128)S(1)} %get-tuple-element.165) | copy-start | bytes 12292
  58.5 27.4 %copy-start.31 = (f32[1,8,128]{2,1,0:T(8,128)}, f32[1,8,128]{2,1,0:T(8,128)S(1)}, u32[]{:S(2)}) copy-start(f32[1,8,128]{2,1,0:T(8,128)S(1)} %get-tuple-element.171) | copy-start | bytes 12292
  59.2 29.3 %copy-start.33 = (f32[1,8,128]{2,1,0:T(8,128)}, f32[1,8,128]{2,1,0:T(8,128)S(1)}, u32[]{:S(2)}) copy-start(f32[1,8,128]{2,1,0:T(8,128)S(1)} %get-tuple-element.174) | copy-start | bytes 12292
  60.4 15.2 %copy-start.37 = (f32[1,8,128]{2,1,0:T(8,128)}, f32[1,8,128]{2,1,0:T(8,128)S(1)}, u32[]{:S(2)}) copy-start(f32[1,8,128]{2,1,0:T(8,128)S(1)} %get-tuple-element.180) | copy-start | bytes 12292
  75.0 14.1 %copy-start.60 = (f32[1,8,128]{2,1,0:T(8,128)}, f32[1,8,128]{2,1,0:T(8,128)S(1)}, u32[]{:S(2)}) copy-start(f32[1,8,128]{2,1,0:T(8,128)S(1)} %get-tuple-element.230) | copy-start | bytes 12292
  90.5 16.8 %copy-start.138 = (f32[4]{0:T(128)S(1)}, f32[4]{0:T(128)}, u32[]{:S(2)}) copy-start(f32[4]{0:T(128)} %constant.50.clone) | copy-start | bytes 52
  110.3 7.6 %copy-start.93 = (f32[8,128]{1,0:T(8,128)S(1)}, f32[8,128]{1,0:T(8,128)}, u32[]{:S(2)}) copy-start(f32[8,128]{1,0:T(8,128)} %get-tuple-element.199) | copy-start | bytes 12292
  110.3 7.6 %copy-start.95 = (f32[8,128]{1,0:T(8,128)S(1)}, f32[8,128]{1,0:T(8,128)}, u32[]{:S(2)}) copy-start(f32[8,128]{1,0:T(8,128)} %get-tuple-element.203) | copy-start | bytes 12292
  110.3 7.6 %copy-start.97 = (f32[8,128]{1,0:T(8,128)S(1)}, f32[8,128]{1,0:T(8,128)}, u32[]{:S(2)}) copy-start(f32[8,128]{1,0:T(8,128)} %get-tuple-element.207) | copy-start | bytes 12292
  110.3 7.6 %copy-start.99 = (f32[8,128]{1,0:T(8,128)S(1)}, f32[8,128]{1,0:T(8,128)}, u32[]{:S(2)}) copy-start(f32[8,128]{1,0:T(8,128)} %get-tuple-element.211) | copy-start | bytes 12292
  110.3 7.6 %copy-start.101 = (f32[8,128]{1,0:T(8,128)S(1)}, f32[8,128]{1,0:T(8,128)}, u32[]{:S(2)}) copy-start(f32[8,128]{1,0:T(8,128)} %get-tuple-element.215) | copy-start | bytes 12292
  110.3 7.6 %copy-start.103 = (f32[8,128]{1,0:T(8,128)S(1)}, f32[8,128]{1,0:T(8,128)}, u32[]{:S(2)}) copy-start(f32[8,128]{1,0:T(8,128)} %get-tuple-element.219) | copy-start | bytes 12292
  110.3 7.6 %copy-start.105 = (f32[8,128]{1,0:T(8,128)S(1)}, f32[8,128]{1,0:T(8,128)}, u32[]{:S(2)}) copy-start(f32[8,128]{1,0:T(8,128)} %get-tuple-element.223) | copy-start | bytes 12292
  110.3 7.6 %copy-start.107 = (f32[8,128]{1,0:T(8,128)S(1)}, f32[8,128]{1,0:T(8,128)}, u32[]{:S(2)}) copy-start(f32[8,128]{1,0:T(8,128)} %get-tuple-element.227) | copy-start | bytes 12292
  110.3 7.6 %copy-start.109 = (f32[8,128]{1,0:T(8,128)S(1)}, f32[8,128]{1,0:T(8,128)}, u32[]{:S(2)}) copy-start(f32[8,128]{1,0:T(8,128)} %get-tuple-element.231) | copy-start | bytes 12292
  110.3 7.6 %copy-start.111 = (f32[8,128]{1,0:T(8,128)S(1)}, f32[8,128]{1,0:T(8,128)}, u32[]{:S(2)}) copy-start(f32[8,128]{1,0:T(8,128)} %get-tuple-element.385) | copy-start | bytes 12292
  110.4 7.6 %copy-start.113 = (f32[8,128]{1,0:T(8,128)S(1)}, f32[8,128]{1,0:T(8,128)}, u32[]{:S(2)}) copy-start(f32[8,128]{1,0:T(8,128)} %get-tuple-element.386) | copy-start | bytes 12292
  110.4 7.6 %copy-start.115 = (f32[8,128]{1,0:T(8,128)S(1)}, f32[8,128]{1,0:T(8,128)}, u32[]{:S(2)}) copy-start(f32[8,128]{1,0:T(8,128)} %get-tuple-element.387) | copy-start | bytes 12292
  110.4 7.6 %copy-start.117 = (f32[8,128]{1,0:T(8,128)S(1)}, f32[8,128]{1,0:T(8,128)}, u32[]{:S(2)}) copy-start(f32[8,128]{1,0:T(8,128)} %get-tuple-element.388) | copy-start | bytes 12292
  110.4 7.6 %copy-start.119 = (f32[8,128]{1,0:T(8,128)S(1)}, f32[8,128]{1,0:T(8,128)}, u32[]{:S(2)}) copy-start(f32[8,128]{1,0:T(8,128)} %get-tuple-element.389) | copy-start | bytes 12292
  125.0 10.8 %collective-permute-start.5 = (f32[320,8,1]{0,1,2:T(8,128)S(1)}, f32[320,8,1]{0,1,2:T(8,128)S(1)}, u32[]{:S(2)}, u32[]{:S(2)}) collective-permute-start(f32[320,8,1]{0,1,2:T(8,128)S(1)} %copy.1385), channel_id=1, source_target_pairs={{1,0},{2,1},{3,2},{4,3},{5,4},{6,5},{7,6},{9,8},{10,9},{11,10},{12... | collective-permute-start | bytes 30728 | tf_op jit(solution)/shard_map/ppermute | solution.py:29
  129.4 6.4 %collective-permute-start.4 = (f32[320,8,1]{0,1,2:T(8,128)S(1)}, f32[320,8,1]{0,1,2:T(8,128)S(1)}, u32[]{:S(2)}, u32[]{:S(2)}) collective-permute-start(f32[320,8,1]{0,1,2:T(8,128)S(1)} %copy.1384), channel_id=1, source_target_pairs={{0,1},{1,2},{2,3},{3,4},{4,5},{5,6},{6,7},{8,9},{9,10},{10,11},{11... | collective-permute-start | bytes 30728 | tf_op jit(solution)/shard_map/ppermute | solution.py:26
  135.9 9.9 %copy-start.3 = (f32[320,8,128]{0,2,1:T(8,128)S(1)}, f32[320,8,128]{0,2,1:T(8,128)}, u32[]{:S(2)}) copy-start(f32[320,8,128]{0,2,1:T(8,128)} %copy.1130) | copy-start | bytes 3932164
  137.1 3.4 %collective-permute-start.7 = (f32[320,1,130]{0,2,1:T(8,128)S(1)}, f32[320,1,130]{0,2,1:T(8,128)S(1)}, u32[]{:S(2)}, u32[]{:S(2)}) collective-permute-start(f32[320,1,130]{0,2,1:T(8,128)S(1)} %get-tuple-element.323), channel_id=1, source_target_pairs={{8,0},{16,8},{24,16},{32,24},{40,32},{48,40},{56,48},{64,56},{72,6... | collective-permute-start | bytes 499208 | tf_op jit(solution)/shard_map/ppermute | solution.py:29
  137.2 8.6 %collective-permute-start.6 = (f32[320,1,130]{0,2,1:T(8,128)S(1)}, f32[320,1,130]{0,2,1:T(8,128)S(1)}, u32[]{:S(2)}, u32[]{:S(2)}) collective-permute-start(f32[320,1,130]{0,2,1:T(8,128)S(1)} %get-tuple-element.322), channel_id=1, source_target_pairs={{0,8},{8,16},{16,24},{24,32},{32,40},{40,48},{48,56},{56,64},{64,7... | collective-permute-start | bytes 499208 | tf_op jit(solution)/shard_map/ppermute | solution.py:26
  165.1 7.5 %copy-start.124 = (f32[8,128]{1,0:T(8,128)S(1)}, f32[8,128]{1,0:T(8,128)}, u32[]{:S(2)}) copy-start(f32[8,128]{1,0:T(8,128)} %get-tuple-element.393) | copy-start | bytes 12292
  165.1 7.5 %copy-start.125 = (f32[8,128]{1,0:T(8,128)S(1)}, f32[8,128]{1,0:T(8,128)}, u32[]{:S(2)}) copy-start(f32[8,128]{1,0:T(8,128)} %get-tuple-element.419) | copy-start | bytes 12292
  165.1 7.5 %copy-start.126 = (f32[8,128]{1,0:T(8,128)S(1)}, f32[8,128]{1,0:T(8,128)}, u32[]{:S(2)}) copy-start(f32[8,128]{1,0:T(8,128)} %get-tuple-element.420) | copy-start | bytes 12292
  165.2 7.5 %copy-start.127 = (f32[8,128]{1,0:T(8,128)S(1)}, f32[8,128]{1,0:T(8,128)}, u32[]{:S(2)}) copy-start(f32[8,128]{1,0:T(8,128)} %get-tuple-element.424) | copy-start | bytes 12292
  165.2 7.5 %copy-start.128 = (f32[8,128]{1,0:T(8,128)S(1)}, f32[8,128]{1,0:T(8,128)}, u32[]{:S(2)}) copy-start(f32[8,128]{1,0:T(8,128)} %get-tuple-element.425) | copy-start | bytes 12292
  165.2 7.5 %copy-start.129 = (f32[8,128]{1,0:T(8,128)S(1)}, f32[8,128]{1,0:T(8,128)}, u32[]{:S(2)}) copy-start(f32[8,128]{1,0:T(8,128)} %get-tuple-element.426) | copy-start | bytes 12292
  165.2 7.5 %copy-start.130 = (f32[8,128]{1,0:T(8,128)S(1)}, f32[8,128]{1,0:T(8,128)}, u32[]{:S(2)}) copy-start(f32[8,128]{1,0:T(8,128)} %get-tuple-element.427) | copy-start | bytes 12292
  165.2 7.5 %copy-start.131 = (f32[8,128]{1,0:T(8,128)S(1)}, f32[8,128]{1,0:T(8,128)}, u32[]{:S(2)}) copy-start(f32[8,128]{1,0:T(8,128)} %get-tuple-element.428) | copy-start | bytes 12292
  (103 other events, 136.2 us)
Sparse Core Ops, SparseCore 0:
  22.1 85.2 reduce-scatter.1
where the time goes:
time: 188 us; the launch traced here: 187 us
  other arithmetic  87.6 us (47%)
  waiting for transfers between devices  34.5 us (18%)
  local copies, waits for them, and re-layouts  27.3 us (15%)
  starting transfers between devices  19.4 us (10%)
  between operations  16.3 us (9%)
    unnamed x80, other arithmetic  21.9 us
    mul x34, other arithmetic, vertical_mix(): following = value_list[level_at] - ratio_list[level_at] * following  20.7 us
    reduce_scatter x1, waiting for transfers between devices, remap_forcing(): lax.psum_scatter(jnp.dot(select, flat_part, precision=lax.Precision.HIGHE...  16.3 us
    div x19, other arithmetic, vertical_mix(): prev_ratio = -upper[level_at] / pivot  11.4 us
    ppermute x4, waiting for transfers between devices, with_halo(): lax.ppermute(lax.slice_in_dim(block, block.shape[dim] - width, None, axis...  10.4 us
    ppermute x4, starting transfers between devices, with_halo(): lax.ppermute(lax.slice_in_dim(block, block.shape[dim] - width, None, axis...  10.4 us
    ppermute x4, starting transfers between devices, with_halo(): lax.ppermute(lax.slice_in_dim(block, 0, width, axis=dim), axis, backward)  8.99 us
    unnamed x364, local copies, waits for them, and re-layouts  8.08 us
  transfers between devices with their start and end apart: 9, of which 5 were waited for; matrix products, arithmetic and copies ran while one was open for 32% of the time, Pallas kernels for 0%

commit v1 on v0

v1 whole, which is shorter than its diff:
```python
import functools

import jax
import jax.numpy as jnp
from jax import lax
from jax.experimental import pallas as pl
from jax.experimental.pallas import tpu as pltpu
from jax.sharding import PartitionSpec as P

DIFFUSE = 0.2
ADVECTION = 0.5
THERMAL = 0.2
HALINE = 0.15
GRAVITY = 0.05
CORIOLIS = 0.3
SURFACE_GAIN = (0.5, 0.4, 0.6, 0.6)

FIELDS = 4
ROWS = 8
LANES = 128
CHUNKS = 4
UNROLL = 4
MSG = FIELDS + 1
MESH = pl.DeviceIdType.MESH


def window(
    n_lon, n_lat, n_comp, levels,
    state, count, rate, flux, weight, target, slot, out,
    raw, cnt, rt, fx, wt, tg, sl,
    grid_q, north_send, row_e, row_w, halo_e, halo_w, halo_n, halo_s, merged,
    part, outbox, inbox, force,
    c0_ref, ib_ref, ab_ref, bb_ref, it_ref, at_ref, bt_ref,
    val, res,
    in_sem, out_sem, halo_send_sem, halo_recv_sem, msg_sem,
):
    per = levels // CHUNKS
    me = lax.axis_index("lon")
    depth = lax.axis_index("lat") * n_comp + lax.axis_index("comp")
    total = n_lat * n_comp
    east = lax.rem(me + 1, n_lon)
    west = lax.rem(me + n_lon - 1, n_lon)
    north = lax.rem(depth + 1, total)
    south = lax.rem(depth + total - 1, total)

    def lon_id(where):
        return {"lon": where}

    def lat_id(where):
        return {"lat": where // n_comp, "comp": lax.rem(where, n_comp)}

    cnt_in = pltpu.make_async_copy(count, cnt, in_sem.at[0])
    cnt_in.start()
    raw_in = []
    for c in range(CHUNKS):
        copy = pltpu.make_async_copy(
            state.at[:, pl.ds(c * per, per)], raw.at[:, pl.ds(c * per, per)], in_sem.at[1 + c]
        )
        copy.start()
        raw_in.append(copy)
    rest_in = []
    for i, (a, b) in enumerate(((target, tg), (slot, sl), (flux, fx), (weight, wt), (rate, rt))):
        copy = pltpu.make_async_copy(a, b, in_sem.at[1 + CHUNKS + i])
        copy.start()
        rest_in.append(copy)

    barrier = pltpu.get_barrier_semaphore()
    pl.semaphore_signal(barrier, inc=1, device_id=lat_id(north), device_id_type=MESH)
    pl.semaphore_signal(barrier, inc=1, device_id=lat_id(south), device_id_type=MESH)

    def greet(d, carry):
        pl.semaphore_signal(
            barrier, inc=1, device_id=lon_id(lax.rem(me + d, n_lon)), device_id_type=MESH
        )
        return carry

    lax.fori_loop(1, n_lon, greet, 0)

    lane = lax.broadcasted_iota(jnp.int32, (ROWS, LANES), 1)
    row = lax.broadcasted_iota(jnp.int32, (ROWS, LANES), 0)
    first_lane, last_lane = lane == 0, lane == LANES - 1
    first_row, last_row = row == 0, row == ROWS - 1
    lane_half = lane // 2
    zero = jnp.zeros((ROWS, LANES), jnp.float32)

    def halo_copies(step, c):
        lo = ROWS + c * FIELDS * per
        size = FIELDS * per
        if step == 0 and c == 0:
            lo, size = 0, size + ROWS
        rows = pl.ds(lo, size)
        made = []
        for i, (src, dst, where) in enumerate((
            (row_e.at[step, rows], halo_w.at[step, rows], lon_id(east)),
            (row_w.at[step, rows], halo_e.at[step, rows], lon_id(west)),
            (north_send.at[step, c], halo_s.at[step, c], lat_id(north)),
            (north_send.at[step, c], halo_n.at[step, c], lat_id(south)),
        )):
            made.append(pltpu.make_async_remote_copy(
                src_ref=src,
                dst_ref=dst,
                send_sem=halo_send_sem.at[step, c, i],
                recv_sem=halo_recv_sem.at[step, c, i],
                device_id=where,
                device_id_type=MESH,
            ))
        return made

    def pack(step, c, kk, fields, packed):
        at = ROWS + (c * per + kk) * FIELDS
        made = []
        for f in range(FIELDS):
            q = fields[f]
            base = ROWS + ((c * per + kk) * FIELDS + f) * ROWS
            grid_q[step, pl.ds(pl.multiple_of(base, ROWS), ROWS), :] = q
            row_w[step, pl.ds(at + f, 1), :] = q[0:1, :]
            row_e[step, pl.ds(at + f, 1), :] = q[ROWS - 1:ROWS, :]
            turned = pltpu.roll(q, 2 * kk + 1, 1)
            made.append(jnp.where(lane_half == kk, turned, packed[f]))
        return tuple(made)

    cnt_in.wait()
    wet_count = cnt[...]
    wet_count_f = wet_count.astype(jnp.float32)
    for step in range(2):
        grid_q[step, pl.ds(0, ROWS), :] = zero
        grid_q[step, pl.ds(ROWS + levels * FIELDS * ROWS, ROWS), :] = zero
    row_w[0, pl.ds(0, ROWS), :] = jnp.broadcast_to(wet_count_f[0:1, :], (ROWS, LANES))
    row_e[0, pl.ds(0, ROWS), :] = jnp.broadcast_to(wet_count_f[ROWS - 1:, :], (ROWS, LANES))
    sends = []
    for c in range(CHUNKS):
        raw_in[c].wait()

        def pack_raw(kk, packed):
            k = c * per + kk
            wet = k < wet_count
            fields = [jnp.where(wet, raw[f, k], zero) for f in range(FIELDS)]
            return pack(0, c, kk, fields, packed)

        packed = lax.fori_loop(0, per, pack_raw, (zero,) * FIELDS, unroll=UNROLL)
        for f in range(FIELDS):
            tile = packed[f]
            if c == 0 and f == 0:
                turned = pltpu.roll(wet_count_f, 2 * per + 1, 1)
                tile = jnp.where(lane_half == per, turned, tile)
            north_send[0, c, f] = tile
        if c == 0:
            pl.semaphore_wait(barrier, n_lon + 1)
        for copy in halo_copies(0, c):
            copy.start()
            sends.append(copy)

    rest_in[0].wait()
    rest_in[1].wait()
    rest_in[2].wait()
    rest_in[3].wait()

    def one_block(b, carry):
        part[b] = jnp.dot(fx[b], wt[b], preferred_element_type=jnp.float32)
        return carry

    lax.fori_loop(0, n_lon, one_block, 0, unroll=UNROLL)
    chosen = (
        lax.broadcasted_iota(jnp.int32, (n_lon, n_lon), 0)
        == jnp.broadcast_to(tg[...], (n_lon, n_lon))
    )
    pick = jnp.where(chosen, 1.0, 0.0).astype(jnp.float32)
    slot_f = jnp.broadcast_to(sl[...].astype(jnp.float32), (n_lon, n_lon))
    for f in range(FIELDS):
        outbox[:, f, :] = jnp.dot(
            pick, part[:, f, :], precision=lax.Precision.HIGHEST,
            preferred_element_type=jnp.float32,
        )
    outbox[:, FIELDS, :] = jnp.dot(
        jnp.where(chosen, slot_f, 0.0), jnp.ones((n_lon, LANES), jnp.float32),
        precision=lax.Precision.HIGHEST, preferred_element_type=jnp.float32,
    )

    def post(d, carry):
        owner = lax.rem(me + d, n_lon)
        pltpu.make_async_remote_copy(
            src_ref=outbox.at[owner],
            dst_ref=inbox.at[me],
            send_sem=msg_sem.at[0],
            recv_sem=msg_sem.at[1],
            device_id=lon_id(owner),
            device_id_type=MESH,
        ).start()
        return carry

    lax.fori_loop(1, n_lon, post, 0)

    rest_in[4].wait()

    def across(k):
        return jnp.where(k + 1 < wet_count, rt[k], zero)

    def factor(i, carry):
        below, inv_b, above, inv_t = carry
        k = levels - 1 - i
        upper = across(jnp.maximum(k - 1, 0))
        upper = jnp.where(k > 0, upper, 0.0)
        inv_b = 1.0 / (1.0 + upper + below - below * below * inv_b)
        masked = jnp.where(k < wet_count, inv_b, 0.0)
        ib_ref[k] = masked
        ab_ref[k] = below * masked
        bb_ref[k] = jnp.where(k > 0, upper, 1.0) * masked
        lower = jnp.where(i < levels - 1, across(i), 0.0)
        inv_t = 1.0 / (1.0 + above + lower - above * above * inv_t)
        masked = jnp.where(i < wet_count, inv_t, 0.0)
        it_ref[i] = masked
        at_ref[i] = jnp.where(i > 0, above, 1.0) * masked
        bt_ref[i] = lower * masked
        return upper, inv_b, lower, inv_t

    lax.fori_loop(0, levels, factor, (zero,) * 4, unroll=UNROLL)

    odd = lax.rem(lane, 2) == 1
    no_north, no_south = depth == total - 1, depth == 0

    def arrive(step, c):
        for copy in halo_copies(step, c):
            copy.wait_recv()
        for f in range(FIELDS):
            from_north = jnp.where(no_north, 0.0, halo_n[step, c, f])
            from_south = jnp.where(no_south, 0.0, halo_s[step, c, f])
            merged[f] = jnp.where(odd, from_north, from_south)

    def lat_pair(q, tile, kk):
        edge = pltpu.roll(tile, LANES - 1 - 2 * kk, 1)
        n = pltpu.roll(jnp.where(first_lane, edge, q), LANES - 1, 1)
        s = pltpu.roll(jnp.where(last_lane, edge, q), 1, 1)
        return n, s

    def row_of(ref, step, at):
        return jnp.broadcast_to(ref[step, pl.ds(at, 1), :], (ROWS, LANES))

    y = (depth * LANES + lane).astype(jnp.float32)
    turning = CORIOLIS * (2.0 * (y + 0.5) / (total * LANES) - 1.0)

    def tendency(step, c, kk, sums, counts):
        k = c * per + kk
        at = ROWS + k * FIELDS
        mid, e, w, n, s = [], [], [], [], []
        for f in range(FIELDS):
            base = ROWS + (k * FIELDS + f) * ROWS
            q = grid_q[step, pl.ds(pl.multiple_of(base, ROWS), ROWS), :]
            e.append(jnp.where(last_row, row_of(halo_e, step, at + f), pltpu.roll(q, ROWS - 1, 0)))
            w.append(jnp.where(first_row, row_of(halo_w, step, at + f), pltpu.roll(q, 1, 0)))
            up, down = lat_pair(q, merged[f], kk)
            n.append(up)
            s.append(down)
            mid.append(q)
        wets = [k < a for a in counts]
        if step == 0:
            shares = [jnp.where(m, DIFFUSE, 0.0) for m in wets]
            c0 = (1.0 - (shares[0] + shares[1])) - (shares[2] + shares[3])
            c0_ref[k] = c0
        else:
            c0 = c0_ref[k]
        half = 0.5 * ADVECTION
        a, b = half * mid[2], half * mid[3]
        to_e, to_w, to_n, to_s = DIFFUSE - a, DIFFUSE + a, DIFFUSE - b, DIFFUSE + b
        new = []
        for f in range(2):
            new.append(
                c0 * mid[f]
                + ((to_e * e[f] + to_w * w[f]) + (to_n * n[f] + to_s * s[f]))
            )
        scale = 0.5 * GRAVITY
        made, pressures = [], []
        for side, m, total_d in zip((e, w, n, s), wets, sums):
            total_d = total_d + (scale * HALINE * side[1] - scale * THERMAL * side[0])
            made.append(total_d)
            pressures.append(jnp.where(m, total_d, 0.0))
        for f, sign, lo, hi in ((2, 1, 1, 0), (3, -1, 3, 2)):
            spread = DIFFUSE * ((e[f] + w[f]) + (n[f] + s[f]))
            twist = turning * mid[5 - f]
            base = c0 * mid[f] + spread
            base = base + twist if sign > 0 else base - twist
            new.append(base - (pressures[hi] - pressures[lo]))
        return new, tuple(made)

    arrive(0, 0)
    count_e = jnp.where(last_row, halo_e[0, pl.ds(0, ROWS), :], pltpu.roll(wet_count_f, ROWS - 1, 0))
    count_w = jnp.where(first_row, halo_w[0, pl.ds(0, ROWS), :], pltpu.roll(wet_count_f, 1, 0))
    count_n, count_s = lat_pair(wet_count_f, merged[0], per)
    counts = [a.astype(jnp.int32) for a in (count_e, count_w, count_n, count_s)]
    sums = (zero,) * 4
    for c in range(CHUNKS):
        if c > 0:
            arrive(0, c)

        def first(kk, sums):
            new, sums = tendency(0, c, kk, sums, counts)
            k = c * per + kk
            ib = ib_ref[k]
            for f in range(FIELDS):
                val[k, f] = ib * new[f]
            return sums

        sums = lax.fori_loop(0, per, first, sums, unroll=UNROLL)

    def upward(i, carry):
        k = levels - 1 - i
        ab = ab_ref[k]
        made = tuple(val[k, f] + ab * carry[f] for f in range(FIELDS))
        for f in range(FIELDS):
            val[k, f] = made[f]
        return made

    lax.fori_loop(0, levels, upward, (zero,) * FIELDS, unroll=UNROLL)

    inbox[me] = outbox[me]
    pltpu.make_async_copy(
        inbox.at[pl.ds(0, n_lon - 1)], inbox.at[pl.ds(0, n_lon - 1)], msg_sem.at[1]
    ).wait()
    row_f = row.astype(jnp.float32)

    def receive(s, carry):
        hit = row_f == jnp.broadcast_to(inbox[s, pl.ds(FIELDS, 1), :], (ROWS, LANES))
        return tuple(
            carry[f]
            + jnp.where(hit, jnp.broadcast_to(inbox[s, pl.ds(f, 1), :], (ROWS, LANES)), 0.0)
            for f in range(FIELDS)
        )

    forced = lax.fori_loop(0, n_lon, receive, (zero,) * FIELDS, unroll=UNROLL)
    for f in range(FIELDS):
        force[f] = SURFACE_GAIN[f] * forced[f]

    carry = tuple(force[f] for f in range(FIELDS))
    for c in range(CHUNKS):

        def downward(kk, carry):
            before, packed = carry
            k = c * per + kk
            bb = bb_ref[k]
            made = tuple(val[k, f] + bb * before[f] for f in range(FIELDS))
            return made, pack(1, c, kk, made, packed)

        carry, packed = lax.fori_loop(0, per, downward, (carry, (zero,) * FIELDS), unroll=UNROLL)
        for f in range(FIELDS):
            north_send[1, c, f] = packed[f]
        for copy in halo_copies(1, c):
            copy.start()
            sends.append(copy)

    sums = (zero,) * 4
    carry = tuple(force[f] for f in range(FIELDS))
    for c in range(CHUNKS):
        arrive(1, c)

        def second(kk, state_in):
            sums, before = state_in
            new, sums = tendency(1, c, kk, sums, counts)
            k = c * per + kk
            it, at = it_ref[k], at_ref[k]
            made = tuple(it * new[f] + at * before[f] for f in range(FIELDS))
            for f in range(FIELDS):
                val[k, f] = made[f]
            return sums, made

        sums, carry = lax.fori_loop(0, per, second, (sums, carry), unroll=UNROLL)

    carry = (zero,) * FIELDS
    outs = []
    for c in reversed(range(CHUNKS)):

        def settle(i, carry):
            k = c * per + per - 1 - i
            bt = bt_ref[k]
            made = tuple(val[k, f] + bt * carry[f] for f in range(FIELDS))
            for f in range(FIELDS):
                res[f, k] = made[f]
            return made

        carry = lax.fori_loop(0, per, settle, carry, unroll=UNROLL)
        copy = pltpu.make_async_copy(
            res.at[:, pl.ds(c * per, per)], out.at[:, pl.ds(c * per, per)], out_sem.at[c]
        )
        copy.start()
        outs.append(copy)
    for copy in outs:
        copy.wait()
    for copy in sends:
        copy.wait_send()
    pltpu.make_async_copy(
        outbox.at[pl.ds(0, n_lon - 1)], outbox.at[pl.ds(0, n_lon - 1)], msg_sem.at[0]
    ).wait()


def local(ocean_state, level_count, mix_rate, atmos_flux, remap_weight, remap_target, remap_slot):
    fields, levels, rows, lanes = ocean_state.shape
    n_lon, n_lat, n_comp = (lax.axis_size(a) for a in ("lon", "lat", "comp"))
    blocks, cells = atmos_flux.shape[1], atmos_flux.shape[3]
    per = levels // CHUNKS
    tile = (levels, rows, lanes)
    f32 = jnp.float32
    row_shape = (2, ROWS + levels * fields, lanes)
    lat_shape = (2, CHUNKS, fields, rows, lanes)
    anywhere = pl.BlockSpec(memory_space=pl.ANY)
    return pl.pallas_call(
        functools.partial(window, n_lon, n_lat, n_comp, levels),
        out_shape=jax.ShapeDtypeStruct(ocean_state.shape, f32),
        in_specs=[anywhere] * 7,
        out_specs=anywhere,
        scratch_shapes=[
            pltpu.VMEM(ocean_state.shape, f32),
            pltpu.VMEM((rows, lanes), jnp.int32),
            pltpu.VMEM(tile, f32),
            pltpu.VMEM((blocks, fields, cells), jnp.bfloat16),
            pltpu.VMEM((blocks, cells, lanes), jnp.bfloat16),
            pltpu.VMEM((1, blocks), jnp.int32),
            pltpu.VMEM((1, blocks), jnp.int32),
            pltpu.VMEM((2, levels * fields * rows + 2 * rows, lanes), f32),
            pltpu.VMEM(lat_shape, f32),
            pltpu.VMEM(row_shape, f32),
            pltpu.VMEM(row_shape, f32),
            pltpu.VMEM(row_shape, f32),
            pltpu.VMEM(row_shape, f32),
            pltpu.VMEM(lat_shape, f32),
            pltpu.VMEM(lat_shape, f32),
            pltpu.VMEM((fields, rows, lanes), f32),
            pltpu.VMEM((blocks, fields, lanes), f32),
            pltpu.VMEM((n_lon, MSG, lanes), f32),
            pltpu.VMEM((n_lon, MSG, lanes), f32),
            pltpu.VMEM((fields, rows, lanes), f32),
        ]
        + [pltpu.VMEM(tile, f32)] * 7
        + [
            pltpu.VMEM((levels, fields, rows, lanes), f32),
            pltpu.VMEM(ocean_state.shape, f32),
            pltpu.SemaphoreType.DMA((1 + CHUNKS + 5,)),
            pltpu.SemaphoreType.DMA((CHUNKS,)),
            pltpu.SemaphoreType.DMA((2, CHUNKS, 4)),
            pltpu.SemaphoreType.DMA((2, CHUNKS, 4)),
            pltpu.SemaphoreType.DMA((2,)),
        ],
        compiler_params=pltpu.CompilerParams(
            collective_id=0, has_side_effects=True, vmem_limit_bytes=48 << 20
        ),
        cost_estimate=pl.CostEstimate(flops=20_000_000, bytes_accessed=5_200_000, transcendentals=0),
    )(
        ocean_state, level_count, mix_rate, atmos_flux[0], remap_weight[0], remap_target, remap_slot
    )


def solution(mesh):
    placed = (
        P(None, None, "lon", ("lat", "comp")),
        P("lon", ("lat", "comp")),
        P(None, "lon", ("lat", "comp")),
        P(("lat", "comp"), "lon", None, None),
        P(("lat", "comp"), "lon", None, None),
        P(("lat", "comp"), "lon"),
        P(("lat", "comp"), "lon"),
    )
    return jax.shard_map(
        local,
        mesh=mesh,
        in_specs=placed,
        out_specs=P(None, None, "lon", ("lat", "comp")),
        check_vma=False,
    )
```

time: 188 us -> 36.2 us (0.19)
  the two profiles are of different devices: /device:TPU:96 before, /device:TPU:1 now
where the time goes in v1:
time: 36.2 us; the launch traced here: 35.9 us
  Pallas kernels  28.1 us (78%)
  local copies, waits for them, and re-layouts  7.77 us (21%)
    pallas_call x1, Pallas kernels, local(): pl.pallas_call(functools.partial(window, n_lon, n_lat, n_comp, levels), o...  28.1 us
    unnamed x15, local copies, waits for them, and re-layouts  7.77 us

profile of v1, /device:TPU:1, one launch (start us, length us, event | category | flops | bytes accessed | tf_op | source)
XLA Modules:
  0.0 35.9 jit_solution(17422948667267748619)
XLA Ops:
  0.0 0.0 copy-start
  0.0 1.6 %copy-done = bf16[1,32,256,128]{3,2,1,0:T(8,128)(2,1)S(1)} copy-done((bf16[1,32,256,128]{3,2,1,0:T(8,128)(2,1)S(1)}, bf16[1,32,256,128]{3,2,1,0:T(8,128)(2,1)}, u32[]{:S(2)}) %copy-start) | copy-done | bytes 2097176
  1.6 0.0 copy-start.1
  1.6 1.3 %copy-done.1 = f32[4,80,8,128]{3,2,1,0:T(8,128)S(1)} copy-done((f32[4,80,8,128]{3,2,1,0:T(8,128)S(1)}, f32[4,80,8,128]{3,2,1,0:T(8,128)}, u32[]{:S(2)}) %copy-start.1) | copy-done | bytes 1310744
  2.9 0.0 copy-start.2
  2.9 1.0 %copy-done.2 = f32[80,8,128]{2,1,0:T(8,128)S(1)} copy-done((f32[80,8,128]{2,1,0:T(8,128)S(1)}, f32[80,8,128]{2,1,0:T(8,128)}, u32[]{:S(2)}) %copy-start.2) | copy-done | bytes 327704
  3.9 0.0 copy-start.3
  3.9 0.8 %copy-done.3 = bf16[1,32,4,256]{3,2,1,0:T(4,128)(2,1)S(1)} copy-done((bf16[1,32,4,256]{3,2,1,0:T(4,128)(2,1)S(1)}, bf16[1,32,4,256]{3,2,1,0:T(4,128)(2,1)}, u32[]{:S(2)}) %copy-start.3) | copy-done | bytes 65560
  4.7 0.0 copy-start.4
  4.7 0.7 %copy-done.4 = s32[8,128]{1,0:T(8,128)S(1)} copy-done((s32[8,128]{1,0:T(8,128)S(1)}, s32[8,128]{1,0:T(8,128)}, u32[]{:S(2)}) %copy-start.4) | copy-done | bytes 4120
  5.4 0.0 copy-start.5
  5.4 0.7 %copy-done.5 = s32[1,32]{1,0:T(1,128)S(1)} copy-done((s32[1,32]{1,0:T(1,128)S(1)}, s32[1,32]{1,0:T(1,128)}, u32[]{:S(2)}) %copy-start.5) | copy-done | bytes 152
  6.1 0.0 copy-start.6
  6.1 0.7 %copy-done.6 = s32[1,32]{1,0:T(1,128)S(1)} copy-done((s32[1,32]{1,0:T(1,128)S(1)}, s32[1,32]{1,0:T(1,128)}, u32[]{:S(2)}) %copy-start.6) | copy-done | bytes 152
  6.7 28.1 %shard_map.73 = f32[4,80,8,128]{3,2,1,0:T(8,128)S(1)} custom-call(f32[4,80,8,128]{3,2,1,0:T(8,128)S(1)} %copy-done.1, s32[8,128]{1,0:T(8,128)S(1)} %copy-done.4, f32[80,8,128]{2,1,0:T(8,128)S(1)} %copy-done.2, bf16[32,4,256]{2,1,0:T(4,128)(2,1)S(1)} %bitcast.3, bf16[32,256,128]{2,1,0:T(8,128)(2,1)S(1)} %bitcast.2, s32[1,32]{1,0:T(1,128)S(1)} %copy-done.5, ...), custom_call_target="tpu_custom_call" | custom-call | flops 20000000 | bytes 5200000 | tf_op jit(solution)/shard_map/pallas_call | solution.py:403
  34.9 1.1 %copy.9 = f32[4,80,8,128]{3,2,1,0:T(8,128)} copy(f32[4,80,8,128]{3,2,1,0:T(8,128)S(1)} %shard_map.73) | data formatting | bytes 2621440
Async XLA Ops:
  0.0 1.6 %copy-start = (bf16[1,32,256,128]{3,2,1,0:T(8,128)(2,1)S(1)}, bf16[1,32,256,128]{3,2,1,0:T(8,128)(2,1)}, u32[]{:S(2)}) copy-start(bf16[1,32,256,128]{3,2,1,0:T(8,128)(2,1)} %param.11) | copy-start | bytes 6291460
  1.6 1.3 %copy-start.1 = (f32[4,80,8,128]{3,2,1,0:T(8,128)S(1)}, f32[4,80,8,128]{3,2,1,0:T(8,128)}, u32[]{:S(2)}) copy-start(f32[4,80,8,128]{3,2,1,0:T(8,128)} %state.1) | copy-start | bytes 3932164
  2.9 1.0 %copy-start.2 = (f32[80,8,128]{2,1,0:T(8,128)S(1)}, f32[80,8,128]{2,1,0:T(8,128)}, u32[]{:S(2)}) copy-start(f32[80,8,128]{2,1,0:T(8,128)} %rate.1) | copy-start | bytes 983044
  3.9 0.8 %copy-start.3 = (bf16[1,32,4,256]{3,2,1,0:T(4,128)(2,1)S(1)}, bf16[1,32,4,256]{3,2,1,0:T(4,128)(2,1)}, u32[]{:S(2)}) copy-start(bf16[1,32,4,256]{3,2,1,0:T(4,128)(2,1)} %param.10) | copy-start | bytes 196612
  4.7 0.7 %copy-start.4 = (s32[8,128]{1,0:T(8,128)S(1)}, s32[8,128]{1,0:T(8,128)}, u32[]{:S(2)}) copy-start(s32[8,128]{1,0:T(8,128)} %count.1) | copy-start | bytes 12292
  5.4 0.7 %copy-start.5 = (s32[1,32]{1,0:T(1,128)S(1)}, s32[1,32]{1,0:T(1,128)}, u32[]{:S(2)}) copy-start(s32[1,32]{1,0:T(1,128)} %target.1) | copy-start | bytes 388
  6.1 0.7 %copy-start.6 = (s32[1,32]{1,0:T(1,128)S(1)}, s32[1,32]{1,0:T(1,128)}, u32[]{:S(2)}) copy-start(s32[1,32]{1,0:T(1,128)} %slot.1) | copy-start | bytes 388

commit v2 on v1

--- a/solution.py
+++ b/solution.py
@@ -19,7 +19,7 @@
 ROWS = 8
 LANES = 128
 CHUNKS = 4
-UNROLL = 4
+UNROLL = 10
 MSG = FIELDS + 1
 MESH = pl.DeviceIdType.MESH
 
@@ -31,8 +31,8 @@
     grid_q, north_send, row_e, row_w, halo_e, halo_w, halo_n, halo_s, merged,
     part, outbox, inbox, force,
     c0_ref, ib_ref, ab_ref, bb_ref, it_ref, at_ref, bt_ref,
-    val, res,
-    in_sem, out_sem, halo_send_sem, halo_recv_sem, msg_sem,
+    val,
+    in_sem, halo_send_sem, halo_recv_sem, msg_sem,
 ):
     per = levels // CHUNKS
     me = lax.axis_index("lon")
@@ -40,8 +40,8 @@
     total = n_lat * n_comp
     east = lax.rem(me + 1, n_lon)
     west = lax.rem(me + n_lon - 1, n_lon)
-    north = lax.rem(depth + 1, total)
-    south = lax.rem(depth + total - 1, total)
+    north = jnp.minimum(depth + 1, total - 1)
+    south = jnp.maximum(depth - 1, 0)
 
     def lon_id(where):
         return {"lon": where}
@@ -65,8 +65,23 @@
         rest_in.append(copy)
 
     barrier = pltpu.get_barrier_semaphore()
-    pl.semaphore_signal(barrier, inc=1, device_id=lat_id(north), device_id_type=MESH)
-    pl.semaphore_signal(barrier, inc=1, device_id=lat_id(south), device_id_type=MESH)
+    has_north, has_south = depth < total - 1, depth > 0
+
+    @pl.when(jnp.logical_not(has_north))
+    def _():
+        halo_n[...] = jnp.zeros_like(halo_n)
+
+    @pl.when(jnp.logical_not(has_south))
+    def _():
+        halo_s[...] = jnp.zeros_like(halo_s)
+
+    @pl.when(has_north)
+    def _():
+        pl.semaphore_signal(barrier, inc=1, device_id=lat_id(north), device_id_type=MESH)
+
+    @pl.when(has_south)
+    def _():
+        pl.semaphore_signal(barrier, inc=1, device_id=lat_id(south), device_id_type=MESH)
 
     def greet(d, carry):
         pl.semaphore_signal(
@@ -106,6 +121,21 @@
             ))
         return made
 
+    def on_sides(made, act):
+        act(made[0])
+        act(made[1])
+
+        @pl.when(has_north)
+        def _():
+            act(made[2])
+
+        @pl.when(has_south)
+        def _():
+            act(made[3])
+
+    def send_halos(step, c):
+        on_sides(halo_copies(step, c), lambda copy: copy.start())
+
     def pack(step, c, kk, fields, packed):
         at = ROWS + (c * per + kk) * FIELDS
         made = []
@@ -127,7 +157,6 @@
         grid_q[step, pl.ds(ROWS + levels * FIELDS * ROWS, ROWS), :] = zero
     row_w[0, pl.ds(0, ROWS), :] = jnp.broadcast_to(wet_count_f[0:1, :], (ROWS, LANES))
     row_e[0, pl.ds(0, ROWS), :] = jnp.broadcast_to(wet_count_f[ROWS - 1:, :], (ROWS, LANES))
-    sends = []
     for c in range(CHUNKS):
         raw_in[c].wait()
 
@@ -145,10 +174,9 @@
                 tile = jnp.where(lane_half == per, turned, tile)
             north_send[0, c, f] = tile
         if c == 0:
-            pl.semaphore_wait(barrier, n_lon + 1)
-        for copy in halo_copies(0, c):
-            copy.start()
-            sends.append(copy)
+            met = n_lon - 1 + has_north.astype(jnp.int32) + has_south.astype(jnp.int32)
+            pl.semaphore_wait(barrier, met)
+        send_halos(0, c)
 
     rest_in[0].wait()
     rest_in[1].wait()
@@ -216,15 +244,22 @@
     lax.fori_loop(0, levels, factor, (zero,) * 4, unroll=UNROLL)
 
     odd = lax.rem(lane, 2) == 1
-    no_north, no_south = depth == total - 1, depth == 0
 
     def arrive(step, c):
-        for copy in halo_copies(step, c):
-            copy.wait_recv()
-        for f in range(FIELDS):
-            from_north = jnp.where(no_north, 0.0, halo_n[step, c, f])
-            from_south = jnp.where(no_south, 0.0, halo_s[step, c, f])
-            merged[f] = jnp.where(odd, from_north, from_south)
+        made = halo_copies(step, c)
+        made[0].wait_recv()
+        made[1].wait_recv()
+
+        @pl.when(has_south)
+        def _():
+            made[2].wait_recv()
+
+        @pl.when(has_north)
+        def _():
+            made[3].wait_recv()
+
+        for f in range(FIELDS):
+            merged[f] = jnp.where(odd, halo_n[step, c, f], halo_s[step, c, f])
 
     def lat_pair(q, tile, kk):
         edge = pltpu.roll(tile, LANES - 1 - 2 * kk, 1)
@@ -342,9 +377,7 @@
         carry, packed = lax.fori_loop(0, per, downward, (carry, (zero,) * FIELDS), unroll=UNROLL)
         for f in range(FIELDS):
             north_send[1, c, f] = packed[f]
-        for copy in halo_copies(1, c):
-            copy.start()
-            sends.append(copy)
+        send_halos(1, c)
 
     sums = (zero,) * 4
     carry = tuple(force[f] for f in range(FIELDS))
@@ -364,7 +397,6 @@
         sums, carry = lax.fori_loop(0, per, second, (sums, carry), unroll=UNROLL)
 
     carry = (zero,) * FIELDS
-    outs = []
     for c in reversed(range(CHUNKS)):
 
         def settle(i, carry):
@@ -372,19 +404,13 @@
             bt = bt_ref[k]
             made = tuple(val[k, f] + bt * carry[f] for f in range(FIELDS))
             for f in range(FIELDS):
-                res[f, k] = made[f]
+                out[f, k] = made[f]
             return made
 
         carry = lax.fori_loop(0, per, settle, carry, unroll=UNROLL)
-        copy = pltpu.make_async_copy(
-            res.at[:, pl.ds(c * per, per)], out.at[:, pl.ds(c * per, per)], out_sem.at[c]
-        )
-        copy.start()
-        outs.append(copy)
-    for copy in outs:
-        copy.wait()
-    for copy in sends:
-        copy.wait_send()
+    for step in range(2):
+        for c in range(CHUNKS):
+            on_sides(halo_copies(step, c), lambda copy: copy.wait_send())
     pltpu.make_async_copy(
         outbox.at[pl.ds(0, n_lon - 1)], outbox.at[pl.ds(0, n_lon - 1)], msg_sem.at[0]
     ).wait()
@@ -399,12 +425,12 @@
     f32 = jnp.float32
     row_shape = (2, ROWS + levels * fields, lanes)
     lat_shape = (2, CHUNKS, fields, rows, lanes)
-    anywhere = pl.BlockSpec(memory_space=pl.ANY)
+    anywhere = pl.BlockSpec(memory_space=pltpu.HBM)
     return pl.pallas_call(
         functools.partial(window, n_lon, n_lat, n_comp, levels),
         out_shape=jax.ShapeDtypeStruct(ocean_state.shape, f32),
         in_specs=[anywhere] * 7,
-        out_specs=anywhere,
+        out_specs=pl.BlockSpec(memory_space=pltpu.VMEM),
         scratch_shapes=[
             pltpu.VMEM(ocean_state.shape, f32),
             pltpu.VMEM((rows, lanes), jnp.int32),
@@ -430,15 +456,13 @@
         + [pltpu.VMEM(tile, f32)] * 7
         + [
             pltpu.VMEM((levels, fields, rows, lanes), f32),
-            pltpu.VMEM(ocean_state.shape, f32),
             pltpu.SemaphoreType.DMA((1 + CHUNKS + 5,)),
-            pltpu.SemaphoreType.DMA((CHUNKS,)),
             pltpu.SemaphoreType.DMA((2, CHUNKS, 4)),
             pltpu.SemaphoreType.DMA((2, CHUNKS, 4)),
             pltpu.SemaphoreType.DMA((2,)),
         ],
         compiler_params=pltpu.CompilerParams(
-            collective_id=0, has_side_effects=True, vmem_limit_bytes=48 << 20
+            collective_id=0, has_side_effects=True, vmem_limit_bytes=60 << 20
         ),
         cost_estimate=pl.CostEstimate(flops=20_000_000, bytes_accessed=5_200_000, transcendentals=0),
     )(

time: 36.2 us -> 24 us (0.66)
  the two profiles are of different devices: /device:TPU:1 before, /device:TPU:96 now
where the time goes in v2:
time: 24 us; the launch traced here: 23.9 us
  Pallas kernels  21.4 us (89%)
  local copies, waits for them, and re-layouts  2.46 us (10%)
    pallas_call x1, Pallas kernels, local(): pl.pallas_call(functools.partial(window, n_lon, n_lat, n_comp, levels), o...  21.4 us
    unnamed x1, local copies, waits for them, and re-layouts  2.46 us

profile of v2, /device:TPU:96, one launch (start us, length us, event | category | flops | bytes accessed | tf_op | source)
XLA Modules:
  0.0 23.9 jit_solution(6958936040473307495)
XLA Ops:
  0.0 21.4 %shard_map.73 = f32[4,80,8,128]{3,2,1,0:T(8,128)} custom-call(f32[4,80,8,128]{3,2,1,0:T(8,128)} %state.1, s32[8,128]{1,0:T(8,128)} %count.1, f32[80,8,128]{2,1,0:T(8,128)} %rate.1, bf16[32,4,256]{2,1,0:T(4,128)(2,1)} %bitcast.3, bf16[32,256,128]{2,1,0:T(8,128)(2,1)} %bitcast.2, s32[1,32]{1,0:T(1,128)} %target.1, s32[1,32]{1,0:T(1,128)} %slot.1), custom_call_target="tpu_custom_call" | custom-call | flops 20000000 | bytes 5200000 | tf_op jit(solution)/shard_map/pallas_call | solution.py:429
  21.4 2.5 %copy.9 = f32[4,80,8,128]{3,2,1,0:T(8,128)} copy(f32[4,80,8,128]{3,2,1,0:T(8,128)} %shard_map.73) | data formatting | bytes 2621440

commit v3 on v2

--- a/solution.py
+++ b/solution.py
@@ -58,12 +58,6 @@
         )
         copy.start()
         raw_in.append(copy)
-    rest_in = []
-    for i, (a, b) in enumerate(((target, tg), (slot, sl), (flux, fx), (weight, wt), (rate, rt))):
-        copy = pltpu.make_async_copy(a, b, in_sem.at[1 + CHUNKS + i])
-        copy.start()
-        rest_in.append(copy)
-
     barrier = pltpu.get_barrier_semaphore()
     has_north, has_south = depth < total - 1, depth > 0
 
@@ -159,6 +153,13 @@
     row_e[0, pl.ds(0, ROWS), :] = jnp.broadcast_to(wet_count_f[ROWS - 1:, :], (ROWS, LANES))
     for c in range(CHUNKS):
         raw_in[c].wait()
+        if c == 0:
+            rest_in = []
+            for i, (a, b) in enumerate(((target, tg), (slot, sl), (flux, fx), (weight, wt), (rate, rt))):
+                copy = pltpu.make_async_copy(a, b, in_sem.at[1 + CHUNKS + i])
+                copy.start()
+                rest_in.append(copy)
+
 
         def pack_raw(kk, packed):
             k = c * per + kk
@@ -462,12 +463,12 @@
             pltpu.SemaphoreType.DMA((2,)),
         ],
         compiler_params=pltpu.CompilerParams(
-            collective_id=0, has_side_effects=True, vmem_limit_bytes=60 << 20
+            collective_id=0, has_side_effects=True, vmem_limit_bytes=40 << 20
         ),
         cost_estimate=pl.CostEstimate(flops=20_000_000, bytes_accessed=5_200_000, transcendentals=0),
-    )(
+    )(*(pltpu.with_memory_space_constraint(x, pltpu.HBM) for x in (
         ocean_state, level_count, mix_rate, atmos_flux[0], remap_weight[0], remap_target, remap_slot
-    )
+    )))
 
 
 def solution(mesh):

time: 24 us -> 21.5 us (0.90)
  local copies, waits for them, and re-layouts: 2.46 us -> 1.06 us
  Pallas kernels: 21.4 us -> 20.3 us
    unnamed x1, local copies, waits for them, and re-layouts: 2.46 us -> 1.06 us
    pallas_call x1, Pallas kernels: 21.4 us -> 20.3 us  [local(): pl.pallas_call(functools.partial(window, n_lon, n_lat, n_comp, levels), o...]
where the time goes in v3:
time: 21.5 us; the launch traced here: 21.3 us
  Pallas kernels  20.3 us (94%)
  local copies, waits for them, and re-layouts  1.06 us (5%)
    pallas_call x1, Pallas kernels, local(): pl.pallas_call(functools.partial(window, n_lon, n_lat, n_comp, levels), o...  20.3 us
    unnamed x1, local copies, waits for them, and re-layouts  1.06 us

profile of v3, /device:TPU:96, one launch (start us, length us, event | category | flops | bytes accessed | tf_op | source)
XLA Modules:
  0.0 21.3 jit_solution(1210163498881422025)
XLA Ops:
  0.0 20.3 %shard_map.73 = f32[4,80,8,128]{3,2,1,0:T(8,128)S(1)} custom-call(f32[4,80,8,128]{3,2,1,0:T(8,128)} %state.1, s32[8,128]{1,0:T(8,128)} %count.1, f32[80,8,128]{2,1,0:T(8,128)} %rate.1, bf16[32,4,256]{2,1,0:T(4,128)(2,1)} %bitcast.3, bf16[32,256,128]{2,1,0:T(8,128)(2,1)} %bitcast.2, s32[1,32]{1,0:T(1,128)} %target.1, s32[1,32]{1,0:T(1,128)} %slot.1), custom_call_target="tpu_custom_call" | custom-call | flops 20000000 | bytes 5200000 | tf_op jit(solution)/shard_map/pallas_call | solution.py:430
  20.3 1.1 %copy.9 = f32[4,80,8,128]{3,2,1,0:T(8,128)} copy(f32[4,80,8,128]{3,2,1,0:T(8,128)S(1)} %shard_map.73) | data formatting | bytes 2621440

commit v4 on v3

--- a/solution.py
+++ b/solution.py
@@ -20,18 +20,18 @@
 LANES = 128
 CHUNKS = 4
 UNROLL = 10
+PIECES = 4
 MSG = FIELDS + 1
 MESH = pl.DeviceIdType.MESH
 
 
 def window(
     n_lon, n_lat, n_comp, levels,
-    state, count, rate, flux, weight, target, slot, out,
+    state, count, rate, flux, weight, target, slot, val, bt_ref,
     raw, cnt, rt, fx, wt, tg, sl,
     grid_q, north_send, row_e, row_w, halo_e, halo_w, halo_n, halo_s, merged,
     part, outbox, inbox, force,
-    c0_ref, ib_ref, ab_ref, bb_ref, it_ref, at_ref, bt_ref,
-    val,
+    c0_ref, ib_ref, ab_ref, bb_ref, it_ref, at_ref,
     in_sem, halo_send_sem, halo_recv_sem, msg_sem,
 ):
     per = levels // CHUNKS
@@ -49,6 +49,33 @@
     def lat_id(where):
         return {"lat": where // n_comp, "comp": lax.rem(where, n_comp)}
 
+    barrier = pltpu.get_barrier_semaphore()
+    has_north, has_south = depth < total - 1, depth > 0
+
+    @pl.when(has_north)
+    def _():
+        pl.semaphore_signal(barrier, inc=1, device_id=lat_id(north), device_id_type=MESH)
+
+    @pl.when(has_south)
+    def _():
+        pl.semaphore_signal(barrier, inc=1, device_id=lat_id(south), device_id_type=MESH)
+
+    def greet(d, carry):
+        pl.semaphore_signal(
+            barrier, inc=1, device_id=lon_id(lax.rem(me + d, n_lon)), device_id_type=MESH
+        )
+        return carry
+
+    lax.fori_loop(1, n_lon, greet, 0)
+
+    @pl.when(jnp.logical_not(has_north))
+    def _():
+        halo_n[...] = jnp.zeros_like(halo_n)
+
+    @pl.when(jnp.logical_not(has_south))
+    def _():
+        halo_s[...] = jnp.zeros_like(halo_s)
+
     cnt_in = pltpu.make_async_copy(count, cnt, in_sem.at[0])
     cnt_in.start()
     raw_in = []
@@ -58,33 +85,6 @@
         )
         copy.start()
         raw_in.append(copy)
-    barrier = pltpu.get_barrier_semaphore()
-    has_north, has_south = depth < total - 1, depth > 0
-
-    @pl.when(jnp.logical_not(has_north))
-    def _():
-        halo_n[...] = jnp.zeros_like(halo_n)
-
-    @pl.when(jnp.logical_not(has_south))
-    def _():
-        halo_s[...] = jnp.zeros_like(halo_s)
-
-    @pl.when(has_north)
-    def _():
-        pl.semaphore_signal(barrier, inc=1, device_id=lat_id(north), device_id_type=MESH)
-
-    @pl.when(has_south)
-    def _():
-        pl.semaphore_signal(barrier, inc=1, device_id=lat_id(south), device_id_type=MESH)
-
-    def greet(d, carry):
-        pl.semaphore_signal(
-            barrier, inc=1, device_id=lon_id(lax.rem(me + d, n_lon)), device_id_type=MESH
-        )
-        return carry
-
-    lax.fori_loop(1, n_lon, greet, 0)
-
     lane = lax.broadcasted_iota(jnp.int32, (ROWS, LANES), 1)
     row = lax.broadcasted_iota(jnp.int32, (ROWS, LANES), 0)
     first_lane, last_lane = lane == 0, lane == LANES - 1
@@ -193,16 +193,22 @@
         lax.broadcasted_iota(jnp.int32, (n_lon, n_lon), 0)
         == jnp.broadcast_to(tg[...], (n_lon, n_lon))
     )
-    pick = jnp.where(chosen, 1.0, 0.0).astype(jnp.float32)
-    slot_f = jnp.broadcast_to(sl[...].astype(jnp.float32), (n_lon, n_lon))
+    pick = jnp.where(chosen, 1.0, 0.0)
+    slot_f = jnp.where(chosen, jnp.broadcast_to(sl[...].astype(jnp.float32), (n_lon, n_lon)), 0.0)
+    half = jnp.bfloat16
+    pick3 = jnp.concatenate([pick, pick, pick], axis=1).astype(half)
     for f in range(FIELDS):
+        whole = part[:, f, :]
+        high = whole.astype(half)
+        rest = whole - high.astype(jnp.float32)
+        middle = rest.astype(half)
+        low = (rest - middle.astype(jnp.float32)).astype(half)
         outbox[:, f, :] = jnp.dot(
-            pick, part[:, f, :], precision=lax.Precision.HIGHEST,
+            pick3, jnp.concatenate([high, middle, low], axis=0),
             preferred_element_type=jnp.float32,
         )
-    outbox[:, FIELDS, :] = jnp.dot(
-        jnp.where(chosen, slot_f, 0.0), jnp.ones((n_lon, LANES), jnp.float32),
-        precision=lax.Precision.HIGHEST, preferred_element_type=jnp.float32,
+    outbox[:, FIELDS, :] = jnp.broadcast_to(
+        jnp.sum(slot_f, axis=1, keepdims=True), (n_lon, LANES)
     )
 
     def post(d, carry):
@@ -397,24 +403,35 @@
 
         sums, carry = lax.fori_loop(0, per, second, (sums, carry), unroll=UNROLL)
 
-    carry = (zero,) * FIELDS
-    for c in reversed(range(CHUNKS)):
-
-        def settle(i, carry):
-            k = c * per + per - 1 - i
-            bt = bt_ref[k]
-            made = tuple(val[k, f] + bt * carry[f] for f in range(FIELDS))
-            for f in range(FIELDS):
-                out[f, k] = made[f]
-            return made
-
-        carry = lax.fori_loop(0, per, settle, carry, unroll=UNROLL)
     for step in range(2):
         for c in range(CHUNKS):
             on_sides(halo_copies(step, c), lambda copy: copy.wait_send())
     pltpu.make_async_copy(
         outbox.at[pl.ds(0, n_lon - 1)], outbox.at[pl.ds(0, n_lon - 1)], msg_sem.at[0]
     ).wait()
+
+
+def finish(levels, val, bt_ref, out, res, sem):
+    per = levels // PIECES
+    carry = (jnp.zeros((ROWS, LANES), jnp.float32),) * FIELDS
+    outs = []
+    for c in reversed(range(PIECES)):
+
+        def settle(i, carry):
+            k = c * per + per - 1 - i
+            bt = bt_ref[k]
+            made = tuple(val[k, f] + bt * carry[f] for f in range(FIELDS))
+            for f in range(FIELDS):
+                res[f, k] = made[f]
+            return made
+
+        carry = lax.fori_loop(0, per, settle, carry, unroll=10)
+        here = pl.ds(c * per, per)
+        copy = pltpu.make_async_copy(res.at[:, here], out.at[:, here], sem.at[c])
+        copy.start()
+        outs.append(copy)
+    for copy in outs:
+        copy.wait()
 
 
 def local(ocean_state, level_count, mix_rate, atmos_flux, remap_weight, remap_target, remap_slot):
@@ -427,11 +444,13 @@
     row_shape = (2, ROWS + levels * fields, lanes)
     lat_shape = (2, CHUNKS, fields, rows, lanes)
     anywhere = pl.BlockSpec(memory_space=pltpu.HBM)
-    return pl.pallas_call(
+    inside = pl.BlockSpec(memory_space=pltpu.VMEM)
+    stack = (levels, fields, rows, lanes)
+    val, bt = pl.pallas_call(
         functools.partial(window, n_lon, n_lat, n_comp, levels),
-        out_shape=jax.ShapeDtypeStruct(ocean_state.shape, f32),
+        out_shape=(jax.ShapeDtypeStruct(stack, f32), jax.ShapeDtypeStruct(tile, f32)),
         in_specs=[anywhere] * 7,
-        out_specs=pl.BlockSpec(memory_space=pltpu.VMEM),
+        out_specs=(inside, inside),
         scratch_shapes=[
             pltpu.VMEM(ocean_state.shape, f32),
             pltpu.VMEM((rows, lanes), jnp.int32),
@@ -454,9 +473,8 @@
             pltpu.VMEM((n_lon, MSG, lanes), f32),
             pltpu.VMEM((fields, rows, lanes), f32),
         ]
-        + [pltpu.VMEM(tile, f32)] * 7
+        + [pltpu.VMEM(tile, f32)] * 6
         + [
-            pltpu.VMEM((levels, fields, rows, lanes), f32),
             pltpu.SemaphoreType.DMA((1 + CHUNKS + 5,)),
             pltpu.SemaphoreType.DMA((2, CHUNKS, 4)),
             pltpu.SemaphoreType.DMA((2, CHUNKS, 4)),
@@ -469,6 +487,19 @@
     )(*(pltpu.with_memory_space_constraint(x, pltpu.HBM) for x in (
         ocean_state, level_count, mix_rate, atmos_flux[0], remap_weight[0], remap_target, remap_slot
     )))
+
+    return pl.pallas_call(
+        functools.partial(finish, levels),
+        out_shape=jax.ShapeDtypeStruct(ocean_state.shape, f32),
+        in_specs=[inside, inside],
+        out_specs=anywhere,
+        scratch_shapes=[
+            pltpu.VMEM(ocean_state.shape, f32),
+            pltpu.SemaphoreType.DMA((PIECES,)),
+        ],
+        compiler_params=pltpu.CompilerParams(vmem_limit_bytes=16 << 20),
+        cost_estimate=pl.CostEstimate(flops=700_000, bytes_accessed=3_000_000, transcendentals=0),
+    )(val, bt)
 
 
 def solution(mesh):

time: 21.5 us -> 21.2 us (0.986)
  local copies, waits for them, and re-layouts: 1.06 us -> 0 us
  Pallas kernels: 20.3 us -> 21 us
    pallas_call x0 -> x1, Pallas kernels: none -> 1.14 us  [local(): pl.pallas_call(functools.partial(finish, levels), out_shape=jax.ShapeDtyp...]
    unnamed x1 -> x0, local copies, waits for them, and re-layouts: 1.06 us -> none
    pallas_call x1, Pallas kernels: 20.3 us -> 19.9 us  [local(): pl.pallas_call(functools.partial(window, n_lon, n_lat, n_comp, levels), o...]
where the time goes in v4:
time: 21.2 us; the launch traced here: 21 us
  Pallas kernels  21 us (99%)
    pallas_call x1, Pallas kernels, local(): pl.pallas_call(functools.partial(window, n_lon, n_lat, n_comp, levels), o...  19.9 us
    pallas_call x1, Pallas kernels, local(): pl.pallas_call(functools.partial(finish, levels), out_shape=jax.ShapeDtyp...  1.14 us

profile of v4, /device:TPU:96, one launch (start us, length us, event | category | flops | bytes accessed | tf_op | source)
XLA Modules:
  0.0 21.0 jit_solution(160368055014569112)
XLA Ops:
  0.0 19.9 %shard_map.73 = (f32[80,4,8,128]{3,2,1,0:T(8,128)S(1)}, f32[80,8,128]{2,1,0:T(8,128)S(1)}) custom-call(f32[4,80,8,128]{3,2,1,0:T(8,128)} %state.1, s32[8,128]{1,0:T(8,128)} %count.1, f32[80,8,128]{2,1,0:T(8,128)} %rate.1, bf16[32,4,256]{2,1,0:T(4,128)(2,1)} %bitcast.3, bf16[32,256,128]{2,1,0:T(8,128)(2,1)} %bitcast.2, s32[1,32]{1,0:T(1,128)} %target.1, ...), custom_call_target="tpu_custom_call" | custom-call | flops 20000000 | bytes 5200000 | tf_op jit(solution)/shard_map/pallas_call | solution.py:449
  19.9 1.1 %shard_map.74 = f32[4,80,8,128]{3,2,1,0:T(8,128)} custom-call(f32[80,4,8,128]{3,2,1,0:T(8,128)S(1)} %get-tuple-element.7.val, f32[80,8,128]{2,1,0:T(8,128)S(1)} %get-tuple-element.8.bt_ref), custom_call_target="tpu_custom_call" | custom-call | flops 700000 | bytes 3000000 | tf_op jit(solution)/shard_map/pallas_call | solution.py:491

commit v5 on v4

--- a/solution.py
+++ b/solution.py
@@ -21,6 +21,7 @@
 CHUNKS = 4
 UNROLL = 10
 PIECES = 4
+ROW = 8
 MSG = FIELDS + 1
 MESH = pl.DeviceIdType.MESH
 
@@ -32,7 +33,7 @@
     grid_q, north_send, row_e, row_w, halo_e, halo_w, halo_n, halo_s, merged,
     part, outbox, inbox, force,
     c0_ref, ib_ref, ab_ref, bb_ref, it_ref, at_ref,
-    in_sem, halo_send_sem, halo_recv_sem, msg_sem,
+    in_sem, halo_send_sem, halo_recv_sem, msg_sem, column_sem,
 ):
     per = levels // CHUNKS
     me = lax.axis_index("lon")
@@ -60,13 +61,35 @@
     def _():
         pl.semaphore_signal(barrier, inc=1, device_id=lat_id(south), device_id_type=MESH)
 
-    def greet(d, carry):
-        pl.semaphore_signal(
-            barrier, inc=1, device_id=lon_id(lax.rem(me + d, n_lon)), device_id_type=MESH
-        )
-        return carry
-
-    lax.fori_loop(1, n_lon, greet, 0)
+    wide = min(ROW, n_lon)
+    tall = n_lon // wide
+    place = lax.rem(me, wide)
+    base = me - place
+
+    def greet(sem, where):
+        pl.semaphore_signal(sem, inc=1, device_id=lon_id(where), device_id_type=MESH)
+
+    def greet_row(sem):
+        def one(d, carry):
+            greet(sem, base + lax.rem(place + d, wide))
+            return carry
+
+        lax.fori_loop(1, wide, one, 0)
+
+    ends_row, starts_row = place == wide - 1, place == 0
+    if tall > 1:
+
+        @pl.when(ends_row)
+        def _():
+            greet(barrier, east)
+
+        @pl.when(starts_row)
+        def _():
+            greet(barrier, west)
+
+        for d in range(1, tall):
+            greet(barrier, lax.rem(me + d * wide, n_lon))
+    greet_row(barrier)
 
     @pl.when(jnp.logical_not(has_north))
     def _():
@@ -175,8 +198,11 @@
                 tile = jnp.where(lane_half == per, turned, tile)
             north_send[0, c, f] = tile
         if c == 0:
-            met = n_lon - 1 + has_north.astype(jnp.int32) + has_south.astype(jnp.int32)
+            met = wide - 1 + has_north.astype(jnp.int32) + has_south.astype(jnp.int32)
+            if tall > 1:
+                met = met + tall - 1 + ends_row.astype(jnp.int32) + starts_row.astype(jnp.int32)
             pl.semaphore_wait(barrier, met)
+            greet_row(column_sem)
         send_halos(0, c)
 
     rest_in[0].wait()
@@ -223,6 +249,7 @@
         ).start()
         return carry
 
+    pl.semaphore_wait(column_sem, wide - 1)
     lax.fori_loop(1, n_lon, post, 0)
 
     rest_in[4].wait()
@@ -479,6 +506,7 @@
             pltpu.SemaphoreType.DMA((2, CHUNKS, 4)),
             pltpu.SemaphoreType.DMA((2, CHUNKS, 4)),
             pltpu.SemaphoreType.DMA((2,)),
+            pltpu.SemaphoreType.REGULAR,
         ],
         compiler_params=pltpu.CompilerParams(
             collective_id=0, has_side_effects=True, vmem_limit_bytes=40 << 20

time: 21.2 us -> 20.7 us (0.976)
  Pallas kernels: 21 us -> 20.6 us
    pallas_call x1, Pallas kernels: 19.9 us -> 19.5 us  [local(): pl.pallas_call(functools.partial(window, n_lon, n_lat, n_comp, levels), o...]
where the time goes in v5:
time: 20.7 us; the launch traced here: 20.6 us
  Pallas kernels  20.6 us (100%)
    pallas_call x1, Pallas kernels, local(): pl.pallas_call(functools.partial(window, n_lon, n_lat, n_comp, levels), o...  19.5 us
    pallas_call x1, Pallas kernels, local(): pl.pallas_call(functools.partial(finish, levels), out_shape=jax.ShapeDtyp...  1.14 us

profile of v5, /device:TPU:96, one launch (start us, length us, event | category | flops | bytes accessed | tf_op | source)
XLA Modules:
  0.0 20.6 jit_solution(16387855570121878015)
XLA Ops:
  0.0 19.5 %shard_map.73 = (f32[80,4,8,128]{3,2,1,0:T(8,128)S(1)}, f32[80,8,128]{2,1,0:T(8,128)S(1)}) custom-call(f32[4,80,8,128]{3,2,1,0:T(8,128)} %state.1, s32[8,128]{1,0:T(8,128)} %count.1, f32[80,8,128]{2,1,0:T(8,128)} %rate.1, bf16[32,4,256]{2,1,0:T(4,128)(2,1)} %bitcast.3, bf16[32,256,128]{2,1,0:T(8,128)(2,1)} %bitcast.2, s32[1,32]{1,0:T(1,128)} %target.1, ...), custom_call_target="tpu_custom_call" | custom-call | flops 20000000 | bytes 5200000 | tf_op jit(solution)/shard_map/pallas_call | solution.py:476
  19.5 1.1 %shard_map.74 = f32[4,80,8,128]{3,2,1,0:T(8,128)} custom-call(f32[80,4,8,128]{3,2,1,0:T(8,128)S(1)} %get-tuple-element.7.val, f32[80,8,128]{2,1,0:T(8,128)S(1)} %get-tuple-element.8.bt_ref), custom_call_target="tpu_custom_call" | custom-call | flops 700000 | bytes 3000000 | tf_op jit(solution)/shard_map/pallas_call | solution.py:519

commit v6 on v5

--- a/solution.py
+++ b/solution.py
@@ -166,6 +166,12 @@
             made.append(jnp.where(lane_half == kk, turned, packed[f]))
         return tuple(made)
 
+    rest_in = []
+    for i, (a, b) in enumerate(((target, tg), (slot, sl), (flux, fx), (weight, wt), (rate, rt))):
+        copy = pltpu.make_async_copy(a, b, in_sem.at[1 + CHUNKS + i])
+        copy.start()
+        rest_in.append(copy)
+
     cnt_in.wait()
     wet_count = cnt[...]
     wet_count_f = wet_count.astype(jnp.float32)
@@ -176,13 +182,6 @@
     row_e[0, pl.ds(0, ROWS), :] = jnp.broadcast_to(wet_count_f[ROWS - 1:, :], (ROWS, LANES))
     for c in range(CHUNKS):
         raw_in[c].wait()
-        if c == 0:
-            rest_in = []
-            for i, (a, b) in enumerate(((target, tg), (slot, sl), (flux, fx), (weight, wt), (rate, rt))):
-                copy = pltpu.make_async_copy(a, b, in_sem.at[1 + CHUNKS + i])
-                copy.start()
-                rest_in.append(copy)
-
 
         def pack_raw(kk, packed):
             k = c * per + kk
@@ -214,7 +213,7 @@
         part[b] = jnp.dot(fx[b], wt[b], preferred_element_type=jnp.float32)
         return carry
 
-    lax.fori_loop(0, n_lon, one_block, 0, unroll=UNROLL)
+    lax.fori_loop(0, n_lon, one_block, 0, unroll=16)
     chosen = (
         lax.broadcasted_iota(jnp.int32, (n_lon, n_lon), 0)
         == jnp.broadcast_to(tg[...], (n_lon, n_lon))
@@ -416,6 +415,14 @@
     sums = (zero,) * 4
     carry = tuple(force[f] for f in range(FIELDS))
     for c in range(CHUNKS):
+        on_sides(halo_copies(0, c), lambda copy: copy.wait_send())
+    pltpu.make_async_copy(
+        outbox.at[pl.ds(0, n_lon - 1)], outbox.at[pl.ds(0, n_lon - 1)], msg_sem.at[0]
+    ).wait()
+    for c in range(CHUNKS):
+        if c == CHUNKS - 1:
+            for sent in range(CHUNKS):
+                on_sides(halo_copies(1, sent), lambda copy: copy.wait_send())
         arrive(1, c)
 
         def second(kk, state_in):
@@ -429,13 +436,6 @@
             return sums, made
 
         sums, carry = lax.fori_loop(0, per, second, (sums, carry), unroll=UNROLL)
-
-    for step in range(2):
-        for c in range(CHUNKS):
-            on_sides(halo_copies(step, c), lambda copy: copy.wait_send())
-    pltpu.make_async_copy(
-        outbox.at[pl.ds(0, n_lon - 1)], outbox.at[pl.ds(0, n_lon - 1)], msg_sem.at[0]
-    ).wait()
 
 
 def finish(levels, val, bt_ref, out, res, sem):

time: 20.7 us -> 20.4 us (0.986)
  Pallas kernels: 20.6 us -> 20.3 us
    pallas_call x1, Pallas kernels: 19.5 us -> 19.2 us  [local(): pl.pallas_call(functools.partial(window, n_lon, n_lat, n_comp, levels), o...]
where the time goes in v6:
time: 20.4 us; the launch traced here: 20.3 us
  Pallas kernels  20.3 us (100%)
    pallas_call x1, Pallas kernels, local(): pl.pallas_call(functools.partial(window, n_lon, n_lat, n_comp, levels), o...  19.2 us
    pallas_call x1, Pallas kernels, local(): pl.pallas_call(functools.partial(finish, levels), out_shape=jax.ShapeDtyp...  1.14 us

profile of v6, /device:TPU:96, one launch (start us, length us, event | category | flops | bytes accessed | tf_op | source)
XLA Modules:
  0.0 20.3 jit_solution(11505637632368972448)
XLA Ops:
  0.0 19.2 %shard_map.73 = (f32[80,4,8,128]{3,2,1,0:T(8,128)S(1)}, f32[80,8,128]{2,1,0:T(8,128)S(1)}) custom-call(f32[4,80,8,128]{3,2,1,0:T(8,128)} %state.1, s32[8,128]{1,0:T(8,128)} %count.1, f32[80,8,128]{2,1,0:T(8,128)} %rate.1, bf16[32,4,256]{2,1,0:T(4,128)(2,1)} %bitcast.3, bf16[32,256,128]{2,1,0:T(8,128)(2,1)} %bitcast.2, s32[1,32]{1,0:T(1,128)} %target.1, ...), custom_call_target="tpu_custom_call" | custom-call | flops 20000000 | bytes 5200000 | tf_op jit(solution)/shard_map/pallas_call | solution.py:476
  19.2 1.1 %shard_map.74 = f32[4,80,8,128]{3,2,1,0:T(8,128)} custom-call(f32[80,4,8,128]{3,2,1,0:T(8,128)S(1)} %get-tuple-element.7.val, f32[80,8,128]{2,1,0:T(8,128)S(1)} %get-tuple-element.8.bt_ref), custom_call_target="tpu_custom_call" | custom-call | flops 700000 | bytes 3000000 | tf_op jit(solution)/shard_map/pallas_call | solution.py:519

commit v7 on v6

--- a/solution.py
+++ b/solution.py
@@ -201,8 +201,9 @@
             if tall > 1:
                 met = met + tall - 1 + ends_row.astype(jnp.int32) + starts_row.astype(jnp.int32)
             pl.semaphore_wait(barrier, met)
+        send_halos(0, c)
+        if c == 0:
             greet_row(column_sem)
-        send_halos(0, c)
 
     rest_in[0].wait()
     rest_in[1].wait()

time: 20.4 us -> 20.4 us (level)
  no operation moved by 1% of the time
where the time goes in v7:
time: 20.4 us; the launch traced here: 20.3 us
  Pallas kernels  20.3 us (100%)
    pallas_call x1, Pallas kernels, local(): pl.pallas_call(functools.partial(window, n_lon, n_lat, n_comp, levels), o...  19.2 us
    pallas_call x1, Pallas kernels, local(): pl.pallas_call(functools.partial(finish, levels), out_shape=jax.ShapeDtyp...  1.14 us

profile of v7, /device:TPU:96, one launch (start us, length us, event | category | flops | bytes accessed | tf_op | source)
XLA Modules:
  0.0 20.3 jit_solution(16677101273377356955)
XLA Ops:
  0.0 19.2 %shard_map.73 = (f32[80,4,8,128]{3,2,1,0:T(8,128)S(1)}, f32[80,8,128]{2,1,0:T(8,128)S(1)}) custom-call(f32[4,80,8,128]{3,2,1,0:T(8,128)} %state.1, s32[8,128]{1,0:T(8,128)} %count.1, f32[80,8,128]{2,1,0:T(8,128)} %rate.1, bf16[32,4,256]{2,1,0:T(4,128)(2,1)} %bitcast.3, bf16[32,256,128]{2,1,0:T(8,128)(2,1)} %bitcast.2, s32[1,32]{1,0:T(1,128)} %target.1, ...), custom_call_target="tpu_custom_call" | custom-call | flops 20000000 | bytes 5200000 | tf_op jit(solution)/shard_map/pallas_call | solution.py:477
  19.2 1.1 %shard_map.74 = f32[4,80,8,128]{3,2,1,0:T(8,128)} custom-call(f32[80,4,8,128]{3,2,1,0:T(8,128)S(1)} %get-tuple-element.7.val, f32[80,8,128]{2,1,0:T(8,128)S(1)} %get-tuple-element.8.bt_ref), custom_call_target="tpu_custom_call" | custom-call | flops 700000 | bytes 3000000 | tf_op jit(solution)/shard_map/pallas_call | solution.py:520
